TPU v7x, 128 devices: a whole 4x4x4 slice. The times are simulated.
128 devices in a mesh: energy: 16 (over y, z_hi, core), section: 8 (over z_lo, x).
Axes of the slice: x: 4, y: 4, z: 4 (z_hi: 2, z_lo: 2; z = z_hi * 2 + z_lo), core: 2. Of those that a mesh axis runs over, the one named last changes fastest.
Arguments:
- self_in: float32 [64, 8, 2, 256, 256], P('energy', 'section'), as said below
- onsite: float32 [8, 256], P('section'), may hold values from -1 to 1
- within: float32 [8, 256, 256], P('section'), may hold values from -0.09375 to 0.09375
- between: float32 [8, 256, 256], P('section'), as said below
- coupling: float32 [8, 256, 256], P('section'), may hold values from -1 to 1
- groups: int32 [8, 256], P('section'), may hold values from 0 to 3
- offsets: int32 [3], replicated, may hold values from 1 to 2, as said below
- strength: float32 [3], replicated, may hold values from 0.3 to 1
Outputs:
- green: float32 [64, 8, 2, 256, 256], P('energy', 'section')
- self_out: float32 [64, 8, 2, 256, 256], P('energy', 'section')
Inputs may be any that keep to these rules, and one draw needn't show every extreme that they name: `offsets`: every entry lies between 1 and 2, and one entry equals 2. `self_in`: imaginary parts of diagonal entries lie between -0.02 and -0.002, real parts of diagonal entries between -0.3 and 0.3; off-diagonal entries lie between -0.01 and 0.01. `between`: diagonal entries lie between 1.4 and 2.0; off-diagonal entries are at most 1.12 / sqrt(256) in magnitude.
All inputs are finite; a program needn't handle non-finite values.
Results may differ from a plain program's by a relative error of at most 0.0001.
Values sent between devices are 32-bit elements; how exact they have to be, the bound alone decides.
No kernel may reach another device: no remote copies, remote signals or barrier semaphores. Data moves between devices by JAX's collectives and lax.ppermute only.
A program may use at most 128 MiB of HBM per device.

v0:
```python
import functools

import jax
import jax.numpy as jnp
from jax import lax
from jax.experimental import pallas as pl
from jax.experimental.pallas import tpu as pltpu
from jax.sharding import PartitionSpec as P


MODES = 3
ETA = 1.0
CONTACT = 0.6
ENERGIES = 64
W = 256
X = 4
AXES = ("energy", "section")
F32 = jnp.float32
BF16 = jnp.bfloat16

LIMIT = 24 << 20


def split(value):
    high = value.astype(BF16)
    return high, (value - high.astype(F32)).astype(BF16)


def dot(left, right):
    return lax.dot_general(left, right, (((1,), (0,)), ((), ())), preferred_element_type=F32)


def dot3(left, right):
    return dot(left[0], right[0]) + (dot(left[0], right[1]) + dot(left[1], right[0]))


def complex_split(real, imag):
    return split(real), split(imag), split(real + imag)


def complex_product(left, right):
    first = dot3(left[0], right[0])
    second = dot3(left[1], right[1])
    third = dot3(left[2], right[2])
    return first - second, third - (first + second)


def on_diagonal():
    rows = lax.broadcasted_iota(jnp.int32, (W, W), 0)
    return rows == lax.broadcasted_iota(jnp.int32, (W, W), 1)


def forward_slab(sys_re, sys_im):
    diagonal = on_diagonal()

    def inverse_diagonal(axis):
        real = jnp.sum(jnp.where(diagonal, sys_re, 0.0), axis=axis, keepdims=True)
        imag = jnp.sum(jnp.where(diagonal, sys_im, 0.0), axis=axis, keepdims=True)
        modulus = real * real + imag * imag
        return real / modulus, -imag / modulus

    col_re, col_im = inverse_diagonal(1)
    row_re, row_im = inverse_diagonal(0)
    r1_re = jnp.where(diagonal, 0.0, col_im * sys_im - col_re * sys_re)
    r1_im = jnp.where(diagonal, 0.0, -(col_re * sys_im + col_im * sys_re))
    r1 = complex_split(r1_re, r1_im)
    r2_re, r2_im = complex_product(r1, r1)
    r2 = complex_split(r2_re, r2_im)
    r3_re, r3_im = complex_product(r2, r1)
    r4_re, r4_im = complex_product(r2, r2)
    sum_re = jnp.where(diagonal, 1.0, 0.0) + r1_re + r2_re + r3_re
    sum_im = r1_im + r2_im + r3_im
    out_re, out_im = complex_product(complex_split(r4_re, r4_im), complex_split(sum_re, sum_im))
    out_re, out_im = out_re + sum_re, out_im + sum_im
    return out_re * row_re - out_im * row_im, out_re * row_im + out_im * row_re


def between_hops(left, value, right):
    return dot3(left, split(dot3(split(value), right)))


def refine(loc_re, loc_im, in_re, in_im):
    local = complex_split(loc_re, loc_im)
    half = complex_split(*complex_product(local, complex_split(in_re, in_im)))
    add_re, add_im = complex_product(half, local)
    return loc_re + add_re, loc_im + add_im


def place():
    section = lax.axis_index("section")
    return section % X, section // X, lax.axis_index("energy") % 2


def system_kernel(self_ref, onsite_ref, within_ref, first_ref, *refs):
    outs, held, hopping, sems = refs[:X], refs[X], refs[X + 1], refs[X + 2]
    x, _, _ = place()

    def order(turn):
        return (2, 1, 3, 0)[turn]

    copies = [pltpu.make_async_copy(within_ref.at[0], hopping, sems.at[X])]
    for place_at in range(X):
        turn = order(place_at)
        copies.append(
            pltpu.make_async_copy(
                self_ref.at[lax.rem(x + turn, X), 0], held.at[turn], sems.at[turn]
            )
        )
    for copy in copies:
        copy.start()
    diagonal = on_diagonal()
    copies[0].wait()
    base = 0.5 * (hopping[...] + hopping[...].T)
    hopping[...] = base + jnp.where(diagonal, onsite_ref[...], 0.0)
    for place_at in range(X):
        turn = order(place_at)
        number = first_ref[0] + lax.rem(x + turn, X)
        energy = -1.0 + (2 * number + 1).astype(F32) / ENERGIES
        copies[1 + place_at].wait()
        outs[turn][0] = jnp.where(diagonal, energy, 0.0) - hopping[...] - held[turn, 0]
        outs[turn][1] = jnp.where(diagonal, ETA, 0.0) - held[turn, 1]


def prepare_kernel(own, direct, swapped, half, other, high, low, high_t, low_t, contact, hops, sems):
    x, _, core = place()
    before, after = lax.rem(x + X - 1, X), lax.rem(x + 1, X)
    far = lax.rem(x + 2, X)
    rows = W // 2
    copies = [
        pltpu.make_async_copy(own.at[0], hops.at[x], sems.at[0]),
        pltpu.make_async_copy(direct, hops.at[jnp.where(core == 0, before, after)], sems.at[1]),
        pltpu.make_async_copy(swapped, hops.at[jnp.where(core == 0, after, before)], sems.at[2]),
        pltpu.make_async_copy(half, hops.at[far, pl.ds(core * rows, rows)], sems.at[3]),
        pltpu.make_async_copy(other, hops.at[far, pl.ds((1 - core) * rows, rows)], sems.at[4]),
    ]
    for copy in copies:
        copy.start()
    for copy in copies:
        copy.wait()
    for slab in range(X):
        high[slab], low[slab] = split(hops[slab])
        high_t[slab], low_t[slab] = split(hops[slab].T)
    contact[...] = CONTACT * dot3((high_t[0], low_t[0]), (high[0], low[0]))


def hop_of(parts, slab):
    return (parts[0][slab], parts[1][slab]), (parts[2][slab], parts[3][slab])


def advance(blocks, slab, parts, prev_re, prev_im):
    hop, hop_t = hop_of(parts, slab)
    sys_re = blocks[slab, 0] - between_hops(hop_t, prev_re, hop)
    sys_im = blocks[slab, 1] - between_hops(hop_t, prev_im, hop)
    return forward_slab(sys_re, sys_im)


def first_kernel(*refs):
    ins, moved, contact, parts, blocks, message, sems = (
        refs[:X], refs[X], refs[X + 1], refs[X + 2 : X + 6], refs[X + 6], refs[X + 7], refs[X + 8],
    )
    x, z, core = place()

    def copy(source, slab):
        return pltpu.make_async_copy(source, blocks.at[slab], sems.at[slab])

    away = (z == 1) & (core == 1)
    for turn in range(X):
        slab = lax.rem(x - turn + X, X)
        if turn == 0:

            @pl.when(away)
            def _(slab=slab):
                copy(moved, slab).start()

            @pl.when(jnp.logical_not(away))
            def _(slab=slab):
                copy(ins[0], slab).start()
        else:
            copy(ins[turn], slab).start()

    @pl.when(z == 1)
    def _():
        for slab in range(X):
            copy(ins[0], slab).wait()

    @pl.when(z == 0)
    def _():
        copy(ins[0], 0).wait()
        blocks[0, 0], blocks[0, 1] = forward_slab(blocks[0, 0], blocks[0, 1] + contact[...])

        def step(slab, unused):
            copy(ins[0], slab).wait()
            real, imag = advance(blocks, slab, parts, blocks[slab - 1, 0], blocks[slab - 1, 1])
            blocks[slab, 0], blocks[slab, 1] = real, imag
            return unused

        lax.fori_loop(1, X, step, 0)
        message[...] = blocks[X - 1]


def second_kernel(mode, *all_refs):
    blocks, message, parts = all_refs[0], all_refs[1], all_refs[2:6]
    refs = all_refs[6 if mode == "middle" else 6 + X :]
    finished = None if mode == "middle" else all_refs[6 : 6 + X]
    if mode == "middle":
        outs, answer, work, carried, sems = refs[:X], refs[X], refs[X + 1], refs[X + 2], refs[X + 3]
    else:
        outs, work, carried, sems = refs[:X], refs[X], refs[X + 1], refs[X + 2]
        far_blocks, far_parts = blocks, parts
        blocks, parts, load_sems = refs[X + 3], refs[X + 4 : X + 8], refs[X + 8]
    x, z, _ = place()

    def loads(slab, hops):
        pairs = [(far_blocks, blocks)] + list(zip(far_parts, parts)) * hops
        return [
            pltpu.make_async_copy(far.at[slab], near.at[slab], load_sems.at[slab, i])
            for i, (far, near) in enumerate(pairs)
        ]

    def put_out(slab):
        for turn in range(X):

            @pl.when(lax.rem(x + turn, X) == slab)
            def _(turn=turn):
                pltpu.make_async_copy(work.at[slab], outs[turn], sems.at[turn]).start()

    def emit(slab, target):
        hop, hop_t = hop_of(parts, slab)
        for part in range(2):
            target[part] = between_hops(hop, work[slab, part], hop_t)

    def retreat(slab, local, incoming):
        real, imag = refine(local[slab, 0], local[slab, 1], incoming[0], incoming[1])
        work[slab, 0], work[slab, 1] = real, imag
        put_out(slab)

    if mode == "last":

        @pl.when(z == 1)
        def _():
            copies = [
                pltpu.make_async_copy(finished[turn], outs[turn], sems.at[turn]) for turn in range(X)
            ]
            for copy in copies:
                copy.start()
            for copy in copies:
                copy.wait()

    @pl.when(z == (1 if mode == "middle" else 0))
    def _():
        if mode == "middle":
            real, imag = advance(blocks, 0, parts, message[0], message[1])
            work[0, 0], work[0, 1] = real, imag

            def forward(slab, unused):
                real, imag = advance(blocks, slab, parts, work[slab - 1, 0], work[slab - 1, 1])
                work[slab, 0], work[slab, 1] = real, imag
                return unused

            lax.fori_loop(1, X, forward, 0)
            put_out(X - 1)
            emit(X - 1, carried)

            def backward(index, unused):
                slab = X - 1 - index
                retreat(slab, work, carried)
                emit(slab, carried)
                return unused

            lax.fori_loop(1, X, backward, 0)
            answer[...] = carried[...]
        else:
            for slab in reversed(range(X)):
                for copy in loads(slab, slab > 0):
                    copy.start()
            carried[...] = message[...]

            def backward(index, unused):
                slab = X - 1 - index
                for copy in loads(slab, True):
                    copy.wait()
                retreat(slab, blocks, carried)
                emit(slab, carried)
                return unused

            lax.fori_loop(0, X - 1, backward, 0)
            for copy in loads(0, False):
                copy.wait()
            retreat(0, blocks, carried)
        for turn in range(X):
            pltpu.make_async_copy(work.at[turn], outs[turn], sems.at[turn]).wait()


ANY = pl.BlockSpec(memory_space=pl.ANY)
VMEM = pl.BlockSpec(memory_space=pltpu.VMEM)
SMEM = pl.BlockSpec(memory_space=pltpu.SMEM)
BLOCK = jax.ShapeDtypeStruct((2, W, W), F32)
MATRIX = jax.ShapeDtypeStruct((W, W), F32)
SLABS4 = jax.ShapeDtypeStruct((X, 2, W, W), F32)
PART = jax.ShapeDtypeStruct((X, W, W), BF16)


def cost(products):
    return pl.CostEstimate(flops=products * 6 * W**3, bytes_accessed=6 << 20, transcendentals=0)


def call(kernel, **options):
    def run(*operands):
        return pl.pallas_call(kernel, **options)(*operands)

    return run


def in_hbm(value):
    return pltpu.with_memory_space_constraint(value, pltpu.HBM)


def first(blocks, moved, contact, parts):
    return call(
        first_kernel,
        out_shape=(SLABS4, BLOCK),
        in_specs=[ANY] * (X + 1) + [VMEM] * 5,
        out_specs=[VMEM] * 2,
        scratch_shapes=[pltpu.SemaphoreType.DMA((X,))],
        name="recursion_first",
        compiler_params=pltpu.CompilerParams(vmem_limit_bytes=LIMIT),
        cost_estimate=cost(64),
    )(*blocks, moved, contact, *parts)


def second(mode, blocks, message, parts, after=()):
    count = X + (mode == "middle")
    near, loaded = VMEM, []
    if mode == "last":
        near = ANY
        blocks, parts = in_hbm(blocks), [in_hbm(part) for part in parts]
        loaded = [pltpu.VMEM((X, 2, W, W), F32)] + [pltpu.VMEM((X, W, W), BF16)] * 4
        loaded.append(pltpu.SemaphoreType.DMA((X, 5)))
    return call(
        functools.partial(second_kernel, mode),
        out_shape=(BLOCK,) * count,
        in_specs=[near, VMEM] + [near] * 4 + [ANY] * len(after),
        out_specs=[VMEM] * count,
        scratch_shapes=[
            pltpu.VMEM((X, 2, W, W), F32),
            pltpu.VMEM((2, W, W), F32),
            pltpu.SemaphoreType.DMA((X,)),
        ]
        + loaded,
        name=f"recursion_{mode}",
        compiler_params=pltpu.CompilerParams(vmem_limit_bytes=LIMIT),
        cost_estimate=cost(104 if mode == "middle" else 40),
    )(blocks, message, *parts, *after)


def scatter_kernel(*refs):
    strength_ref, offsets_ref, coupling_ref, groups_ref = refs[:4]
    blocks, halos = refs[4 : 4 + X], refs[4 + X : 4 + 2 * X]
    green_ref, self_ref = refs[4 + 2 * X : 6 + 2 * X]
    own, side, out, in_sems, out_sems = refs[6 + 2 * X :]
    x, _, _ = place()
    for turn in range(X):
        index = lax.rem(x - turn + X, X)
        pltpu.make_async_copy(blocks[turn], own.at[index], in_sems.at[index]).start()
        pltpu.make_async_copy(halos[turn], side.at[index], in_sems.at[X + index]).start()

    weights = []
    for distance in (1, 2):
        weights.append(
            sum(
                jnp.where(offsets_ref[mode] == distance, strength_ref[mode], 0.0)
                for mode in range(MODES)
            )
        )
    groups = jnp.broadcast_to(groups_ref[...], (W, W)).astype(F32)
    matrix = jnp.where(groups == groups.T, coupling_ref[0], 0.0)
    left, right = split(matrix), split(matrix.T)
    store = []
    for index in range(X):
        pltpu.make_async_copy(blocks[0], own.at[index], in_sems.at[index]).wait()
        copy = pltpu.make_async_copy(own.at[index], green_ref.at[index, 0], out_sems.at[index])
        copy.start()
        store.append(copy)
    for index in range(X):
        pltpu.make_async_copy(blocks[0], side.at[index], in_sems.at[X + index]).wait()

    def energy(index):
        return side[index + X] if index < 0 else own[index] if index < X else side[index - X]

    for index in range(X):
        near = energy(index - 1) + energy(index + 1)
        far = energy(index - 2) + energy(index + 2)
        total = weights[0] * near + weights[1] * far
        for part in range(2):
            out[index, part] = between_hops(left, total[part], right)
        copy = pltpu.make_async_copy(out.at[index], self_ref.at[index, 0], out_sems.at[X + index])
        copy.start()
        store.append(copy)
    for copy in store:
        copy.wait()


def send(value, pairs):
    return lax.ppermute(value, AXES, pairs)


def per_device(self_in, onsite, within, between, coupling, groups, offsets, strength):
    count, sections = lax.axis_size("energy"), lax.axis_size("section")
    _, _, core = place()
    chunks, lanes = range(count), range(sections)

    def device(chunk, section):
        return chunk * sections + section

    def shifted(section, turn):
        return section // X * X + (section + turn) % X

    def host(chunk, section):
        return chunk ^ 2 if section >= X and chunk % 2 else chunk

    half = lax.dynamic_slice_in_dim(between[0], core * (W // 2), W // 2, 0)
    direct = send(
        between[0],
        [(device(c, s), device(c, shifted(s, 1 if c % 2 == 0 else -1))) for c in chunks for s in lanes],
    )
    far = send(half, [(device(c, s), device(c, shifted(s, 2))) for c in chunks for s in lanes])
    partner = [(device(c, s), device(c ^ 1, s)) for c in chunks for s in lanes]
    received = (between, direct, send(direct, partner), far, send(far, partner))
    *parts, contact = call(
        prepare_kernel,
        out_shape=(PART,) * 4 + (MATRIX,),
        in_specs=[ANY] * 5,
        out_specs=[VMEM] * 5,
        scratch_shapes=[pltpu.VMEM((X, W, W), F32), pltpu.SemaphoreType.DMA((5,))],
        name="prepare",
        compiler_params=pltpu.CompilerParams(vmem_limit_bytes=LIMIT),
        cost_estimate=cost(1),
    )(*received)

    first_index = (lax.axis_index("energy") * X).reshape(1)
    systems = call(
        system_kernel,
        out_shape=(BLOCK,) * X,
        in_specs=[ANY, VMEM, ANY, SMEM],
        out_specs=[VMEM] * X,
        scratch_shapes=[
            pltpu.VMEM((X, 2, W, W), F32),
            pltpu.VMEM((W, W), F32),
            pltpu.SemaphoreType.DMA((X + 1,)),
        ],
        name="systems",
        compiler_params=pltpu.CompilerParams(vmem_limit_bytes=LIMIT),
    )(in_hbm(self_in), onsite, in_hbm(within), first_index)

    def exchange(values, back):
        result = []
        for turn in range(X):
            pairs = []
            for c in chunks:
                for s in lanes:
                    if turn or back or host(c, s) != c:
                        ends = (host(c, s), c) if back else (c, host(c, s))
                        pairs.append((device(ends[0], s), device(ends[1], shifted(s, turn))))
            result.append(send(values[turn], pairs))
        return result

    def halo(values):
        result = []
        for turn in range(X):
            pairs = []
            for c in chunks:
                for s in lanes:
                    target = c - 1 if (s - turn) % X < 2 else c + 1
                    if 0 <= target < count:
                        pairs.append((device(c, s), device(target, s)))
            result.append(send(values[turn], pairs))
        return result

    up = [(device(c, s), device(host(c, s + X), s + X)) for c in chunks for s in range(X)]
    down = [(target, source) for source, target in up]
    moved, *others = exchange(systems, False)
    lined_up, message = first((systems[0], *others), moved, contact, parts)
    message = send(message, up)
    *greens, message = second("middle", lined_up, message, parts)
    message = send(message, down)
    greens = second("last", lined_up, message, parts, greens)
    greens = exchange(greens, True)
    halos = halo(greens)

    return call(
        scatter_kernel,
        out_shape=(
            jax.ShapeDtypeStruct((X, 1, 2, W, W), F32),
            jax.ShapeDtypeStruct((X, 1, 2, W, W), F32),
        ),
        in_specs=[SMEM, SMEM, VMEM, VMEM] + [ANY] * (2 * X),
        out_specs=[ANY, ANY],
        scratch_shapes=[
            pltpu.VMEM((X, 2, W, W), F32),
            pltpu.VMEM((X, 2, W, W), F32),
            pltpu.VMEM((X, 2, W, W), F32),
            pltpu.SemaphoreType.DMA((2 * X,)),
            pltpu.SemaphoreType.DMA((2 * X,)),
        ],
        name="scatter",
        compiler_params=pltpu.CompilerParams(vmem_limit_bytes=LIMIT),
        cost_estimate=cost(16),
    )(strength, offsets, coupling, groups, *greens, *halos)


def solution(mesh):
    placed = (
        P("energy", "section", None, None, None),
        P("section", None),
        P("section", None, None),
        P("section", None, None),
        P("section", None, None),
        P("section", None),
        P(),
        P(),
    )


    def step(*arguments):
        return per_device(*arguments)

    step = jax.shard_map(
        step,
        mesh=mesh,
        in_specs=placed,
        out_specs=(
            P("energy", "section", None, None, None),
            P("energy", "section", None, None, None),
        ),
        check_vma=False,
    )
    return step
```

profile of v0, /device:TPU:1, one launch (start us, length us, event | category | flops | bytes accessed | tf_op | source)
XLA Modules:
  0.0 143.6 jit_solution(4644025516902737899)
XLA Ops:
  0.7 1.0 dynamic-slice_bitcast_fusion
  1.6 3.6 %collective-permute-start.6 = (f32[128,256]{1,0:T(8,128)S(1)}, f32[128,256]{1,0:T(8,128)S(1)}, u32[]{:S(2)}, u32[]{:S(2)}) collective-permute-start(f32[128,256]{1,0:T(8,128)S(1)} %dynamic-slice_bitcast_fusion), channel_id=1, source_target_pairs={{0,2},{1,3},{2,0},{3,1},{4,6},{5,7},{6,4},{7,5},{8,10},{9,11},{10,... | collective-permute-start | bytes 393224 | tf_op jit(solution)/shard_map/ppermute | solution.py:404
  5.3 2.8 %collective-permute-done.6.half = f32[128,256]{1,0:T(8,128)S(1)} collective-permute-done((f32[128,256]{1,0:T(8,128)S(1)}, f32[128,256]{1,0:T(8,128)S(1)}, u32[]{:S(2)}, u32[]{:S(2)}) %collective-permute-start.6) | collective-permute-done | bytes 131104 | tf_op jit(solution)/shard_map/ppermute | solution.py:404
  8.1 1.6 %collective-permute-start.7 = (f32[128,256]{1,0:T(8,128)S(1)}, f32[128,256]{1,0:T(8,128)S(1)}, u32[]{:S(2)}, u32[]{:S(2)}) collective-permute-start(f32[128,256]{1,0:T(8,128)S(1)} %collective-permute-done.6.half), channel_id=1, source_target_pairs={{0,8},{1,9},{2,10},{3,11},{4,12},{5,13},{6,14},{7,15},{8,0},{9,1},... | collective-permute-start | bytes 393224 | tf_op jit(solution)/shard_map/ppermute | solution.py:404
  9.7 2.7 %collective-permute-start.4 = (f32[256,256]{1,0:T(8,128)}, f32[256,256]{1,0:T(8,128)S(1)}, u32[]{:S(2)}, u32[]{:S(2)}) collective-permute-start(f32[256,256]{1,0:T(8,128)} %bitcast.4), channel_id=1, source_target_pairs={{0,1},{1,2},{2,3},{3,0},{4,5},{5,6},{6,7},{7,4},{8,11},{9,8},{10,9... | collective-permute-start | bytes 786440 | tf_op jit(solution)/shard_map/ppermute | solution.py:404
  12.4 0.7 copy-done.1
  13.1 1.7 %systems.1 = (f32[2,256,256]{2,1,0:T(8,128)S(1)}, f32[2,256,256]{2,1,0:T(8,128)S(1)}, f32[2,256,256]{2,1,0:T(8,128)S(1)}, f32[2,256,256]{2,1,0:T(8,128)S(1)}) custom-call(f32[4,1,2,256,256]{4,3,2,1,0:T(8,128)} %self_ref.1, f32[1,256]{1,0:T(1,128)S(1)} %copy-done.1, f32[1,256,256]{2,1,0:T(8,128)} %within_ref.1, s32[1]{0:T(128)} %bitcast.first_ref), custom_call_target="tpu_custom_call" | custom-call | tf_op jit(solution)/shard_map/systems/pallas_call | solution.py:309
  14.9 1.7 %collective-permute-start.1 = (f32[2,256,256]{2,1,0:T(8,128)S(1)}, f32[2,256,256]{2,1,0:T(8,128)S(1)}, u32[]{:S(2)}, u32[]{:S(2)}) collective-permute-start(f32[2,256,256]{2,1,0:T(8,128)S(1)} %get-tuple-element.24), channel_id=1, source_target_pairs={{0,2},{1,3},{2,0},{3,1},{4,6},{5,7},{6,4},{7,5},{8,10},{9,11},{10,... | collective-permute-start | bytes 1572872 | tf_op jit(solution)/shard_map/ppermute | solution.py:404
  16.6 0.9 collective-permute-start.2
  17.5 0.7 collective-permute-start.3
  18.2 1.8 %collective-permute-start.5 = (f32[256,256]{1,0:T(8,128)S(1)}, f32[256,256]{1,0:T(8,128)S(1)}, u32[]{:S(2)}, u32[]{:S(2)}) collective-permute-start(f32[256,256]{1,0:T(8,128)S(1)} %collective-permute-done.4.direct), channel_id=1, source_target_pairs={{0,8},{1,9},{2,10},{3,11},{4,12},{5,13},{6,14},{7,15},{8,0},{9,1},... | collective-permute-start | bytes 786440 | tf_op jit(solution)/shard_map/ppermute | solution.py:404
  20.0 1.2 collective-permute-done.5.swapped
  21.2 0.9 prepare.1
  22.2 7.4 %collective-permute-done.refs_1_ = f32[2,256,256]{2,1,0:T(8,128)S(1)} collective-permute-done((f32[2,256,256]{2,1,0:T(8,128)S(1)}, f32[2,256,256]{2,1,0:T(8,128)S(1)}, u32[]{:S(2)}, u32[]{:S(2)}) %collective-permute-start) | collective-permute-done | bytes 524320 | tf_op jit(solution)/shard_map/ppermute | solution.py:404
  29.6 10.7 %collective-permute-done.1.refs_2_ = f32[2,256,256]{2,1,0:T(8,128)S(1)} collective-permute-done((f32[2,256,256]{2,1,0:T(8,128)S(1)}, f32[2,256,256]{2,1,0:T(8,128)S(1)}, u32[]{:S(2)}, u32[]{:S(2)}) %collective-permute-start.1) | collective-permute-done | bytes 524320 | tf_op jit(solution)/shard_map/ppermute | solution.py:404
  40.3 1.1 collective-permute-done.2.refs_3_
  41.4 9.8 %recursion_first.1 = (f32[4,2,256,256]{3,2,1,0:T(8,128)S(1)}, f32[2,256,256]{2,1,0:T(8,128)S(1)}) custom-call(f32[2,256,256]{2,1,0:T(8,128)S(1)} %get-tuple-element.22.refs_0_, f32[2,256,256]{2,1,0:T(8,128)S(1)} %collective-permute-done.refs_1_, f32[2,256,256]{2,1,0:T(8,128)S(1)} %collective-permute-done.1.refs_2_, ...), custom_call_target="tpu_custom_call" | custom-call | flops 6442450944 | bytes 6291456 | tf_op jit(solution)/shard_map/recursion_first/pallas_call | solution.py:309
  51.2 1.3 collective-permute-start.8
  52.6 6.1 %collective-permute-done.8.all_refs_1_ = f32[2,256,256]{2,1,0:T(8,128)S(1)} collective-permute-done((f32[2,256,256]{2,1,0:T(8,128)S(1)}, f32[2,256,256]{2,1,0:T(8,128)S(1)}, u32[]{:S(2)}, u32[]{:S(2)}) %collective-permute-start.8) | collective-permute-done | bytes 524320 | tf_op jit(solution)/shard_map/ppermute | solution.py:404
  58.9 1.3 collective-permute-start.9
  60.2 26.4 %collective-permute-done.9.all_refs_1_ = f32[2,256,256]{2,1,0:T(8,128)S(1)} collective-permute-done((f32[2,256,256]{2,1,0:T(8,128)S(1)}, f32[2,256,256]{2,1,0:T(8,128)S(1)}, u32[]{:S(2)}, u32[]{:S(2)}) %collective-permute-start.9) | collective-permute-done | bytes 524320 | tf_op jit(solution)/shard_map/ppermute | solution.py:404
  86.6 7.8 %recursion_last.1 = (f32[2,256,256]{2,1,0:T(8,128)S(1)}, f32[2,256,256]{2,1,0:T(8,128)S(1)}, f32[2,256,256]{2,1,0:T(8,128)S(1)}, f32[2,256,256]{2,1,0:T(8,128)S(1)}) custom-call(f32[4,2,256,256]{3,2,1,0:T(8,128)} %copy-done.10, f32[2,256,256]{2,1,0:T(8,128)S(1)} %collective-permute-done.9.all_refs_1_, bf16[4,256,256]{2,1,0:T(8,128)(2,1)} %copy-done.2, ...), custom_call_target="tpu_custom_call" | custom-call | flops 4026531840 | bytes 6291456 | tf_op jit(solution)/shard_map/recursion_last/pallas_call | solution.py:309
  94.4 0.7 collective-permute-start.10
  95.6 3.1 %collective-permute-start.12 = (f32[2,256,256]{2,1,0:T(8,128)S(1)}, f32[2,256,256]{2,1,0:T(8,128)S(1)}, u32[]{:S(2)}, u32[]{:S(2)}) collective-permute-start(f32[2,256,256]{2,1,0:T(8,128)S(1)} %get-tuple-element.40), channel_id=1, source_target_pairs={{0,2},{1,3},{2,0},{3,1},{4,6},{5,7},{6,4},{7,5},{8,10},{9,11},{10,... | collective-permute-start | bytes 1572872 | tf_op jit(solution)/shard_map/ppermute | solution.py:404
  98.7 3.5 %collective-permute-start.14 = (f32[2,256,256]{2,1,0:T(8,128)S(1)}, f32[2,256,256]{2,1,0:T(8,128)S(1)}, u32[]{:S(2)}, u32[]{:S(2)}) collective-permute-start(f32[2,256,256]{2,1,0:T(8,128)S(1)} %collective-permute-done.10.refs_4_), channel_id=1, source_target_pairs={{2,10},{3,11},{6,14},{7,15},{8,0},{9,1},{10,18},{11,19},{12,4},{13... | collective-permute-start | bytes 1572872 | tf_op jit(solution)/shard_map/ppermute | solution.py:404
  102.3 6.7 %collective-permute-done.11.refs_5_ = f32[2,256,256]{2,1,0:T(8,128)S(1)} collective-permute-done((f32[2,256,256]{2,1,0:T(8,128)S(1)}, f32[2,256,256]{2,1,0:T(8,128)S(1)}, u32[]{:S(2)}, u32[]{:S(2)}) %collective-permute-start.11) | collective-permute-done | bytes 524320 | tf_op jit(solution)/shard_map/ppermute | solution.py:404
  108.9 7.8 %collective-permute-start.15 = (f32[2,256,256]{2,1,0:T(8,128)S(1)}, f32[2,256,256]{2,1,0:T(8,128)S(1)}, u32[]{:S(2)}, u32[]{:S(2)}) collective-permute-start(f32[2,256,256]{2,1,0:T(8,128)S(1)} %collective-permute-done.11.refs_5_), channel_id=1, source_target_pairs={{0,8},{3,11},{4,12},{7,15},{8,16},{9,1},{10,2},{11,19},{12,20},{13... | collective-permute-start | bytes 1572872 | tf_op jit(solution)/shard_map/ppermute | solution.py:404
  116.7 4.2 %collective-permute-done.12.refs_6_ = f32[2,256,256]{2,1,0:T(8,128)S(1)} collective-permute-done((f32[2,256,256]{2,1,0:T(8,128)S(1)}, f32[2,256,256]{2,1,0:T(8,128)S(1)}, u32[]{:S(2)}, u32[]{:S(2)}) %collective-permute-start.12) | collective-permute-done | bytes 524320 | tf_op jit(solution)/shard_map/ppermute | solution.py:404
  120.9 6.4 %collective-permute-start.16 = (f32[2,256,256]{2,1,0:T(8,128)S(1)}, f32[2,256,256]{2,1,0:T(8,128)S(1)}, u32[]{:S(2)}, u32[]{:S(2)}) collective-permute-start(f32[2,256,256]{2,1,0:T(8,128)S(1)} %collective-permute-done.12.refs_6_), channel_id=1, source_target_pairs={{0,8},{1,9},{4,12},{5,13},{8,16},{9,17},{10,2},{11,3},{12,20},{13,... | collective-permute-start | bytes 1572872 | tf_op jit(solution)/shard_map/ppermute | solution.py:404
  127.3 1.9 %collective-permute-start.17 = (f32[2,256,256]{2,1,0:T(8,128)S(1)}, f32[2,256,256]{2,1,0:T(8,128)S(1)}, u32[]{:S(2)}, u32[]{:S(2)}) collective-permute-start(f32[2,256,256]{2,1,0:T(8,128)S(1)} %collective-permute-done.13.refs_7_), channel_id=1, source_target_pairs={{1,9},{2,10},{5,13},{6,14},{8,0},{9,17},{10,18},{11,3},{12,4},{13,... | collective-permute-start | bytes 1572872 | tf_op jit(solution)/shard_map/ppermute | solution.py:404
  129.3 9.8 %collective-permute-done.16.refs_10_ = f32[2,256,256]{2,1,0:T(8,128)S(1)} collective-permute-done((f32[2,256,256]{2,1,0:T(8,128)S(1)}, f32[2,256,256]{2,1,0:T(8,128)S(1)}, u32[]{:S(2)}, u32[]{:S(2)}) %collective-permute-start.16) | collective-permute-done | bytes 524320 | tf_op jit(solution)/shard_map/ppermute | solution.py:404
  139.3 4.1 %scatter.1 = (f32[4,1,2,256,256]{4,3,2,1,0:T(8,128)}, f32[4,1,2,256,256]{4,3,2,1,0:T(8,128)}) custom-call(f32[3]{0:T(128)S(1)} %copy-done.8, s32[3]{0:T(128)S(1)} %copy-done.9, f32[1,256,256]{2,1,0:T(8,128)S(1)} %copy-done.6, s32[1,256]{1,0:T(1,128)S(1)} %copy-done.7, f32[2,256,256]{2,1,0:T(8,128)S(1)} %collective-permute-done.10.refs_4_, ...), custom_call_target="tpu_custom_call" | custom-call | flops 1610612736 | bytes 6291456 | tf_op jit(solution)/shard_map/scatter/pallas_call | solution.py:309
  (33 shorter events, 1.2 us)
Async XLA Ops:
  0.6 20.6 %copy-start = (f32[1,256,256]{2,1,0:T(8,128)S(1)}, f32[1,256,256]{2,1,0:T(8,128)}, u32[]{:S(2)}) copy-start(f32[1,256,256]{2,1,0:T(8,128)} %own.1) | copy-start | bytes 786436
  1.6 6.5 %collective-permute-start.6 = (f32[128,256]{1,0:T(8,128)S(1)}, f32[128,256]{1,0:T(8,128)S(1)}, u32[]{:S(2)}, u32[]{:S(2)}) collective-permute-start(f32[128,256]{1,0:T(8,128)S(1)} %dynamic-slice_bitcast_fusion), channel_id=1, source_target_pairs={{0,2},{1,3},{2,0},{3,1},{4,6},{5,7},{6,4},{7,5},{8,10},{9,11},{10,... | collective-permute-start | bytes 393224 | tf_op jit(solution)/shard_map/ppermute | solution.py:404
  8.1 9.5 %collective-permute-start.7 = (f32[128,256]{1,0:T(8,128)S(1)}, f32[128,256]{1,0:T(8,128)S(1)}, u32[]{:S(2)}, u32[]{:S(2)}) collective-permute-start(f32[128,256]{1,0:T(8,128)S(1)} %collective-permute-done.6.half), channel_id=1, source_target_pairs={{0,8},{1,9},{2,10},{3,11},{4,12},{5,13},{6,14},{7,15},{8,0},{9,1},... | collective-permute-start | bytes 393224 | tf_op jit(solution)/shard_map/ppermute | solution.py:404
  9.7 8.5 %collective-permute-start.4 = (f32[256,256]{1,0:T(8,128)}, f32[256,256]{1,0:T(8,128)S(1)}, u32[]{:S(2)}, u32[]{:S(2)}) collective-permute-start(f32[256,256]{1,0:T(8,128)} %bitcast.4), channel_id=1, source_target_pairs={{0,1},{1,2},{2,3},{3,0},{4,5},{5,6},{6,7},{7,4},{8,11},{9,8},{10,9... | collective-permute-start | bytes 786440 | tf_op jit(solution)/shard_map/ppermute | solution.py:404
  12.4 0.7 copy-start.1
  14.8 14.8 %collective-permute-start = (f32[2,256,256]{2,1,0:T(8,128)S(1)}, f32[2,256,256]{2,1,0:T(8,128)S(1)}, u32[]{:S(2)}, u32[]{:S(2)}) collective-permute-start(f32[2,256,256]{2,1,0:T(8,128)S(1)} %get-tuple-element.23), channel_id=1, source_target_pairs={{0,1},{1,2},{2,3},{3,0},{4,5},{5,6},{6,7},{7,4},{8,9},{9,10},{10,1... | collective-permute-start | bytes 1572872 | tf_op jit(solution)/shard_map/ppermute | solution.py:404
  14.9 25.4 %collective-permute-start.1 = (f32[2,256,256]{2,1,0:T(8,128)S(1)}, f32[2,256,256]{2,1,0:T(8,128)S(1)}, u32[]{:S(2)}, u32[]{:S(2)}) collective-permute-start(f32[2,256,256]{2,1,0:T(8,128)S(1)} %get-tuple-element.24), channel_id=1, source_target_pairs={{0,2},{1,3},{2,0},{3,1},{4,6},{5,7},{6,4},{7,5},{8,10},{9,11},{10,... | collective-permute-start | bytes 1572872 | tf_op jit(solution)/shard_map/ppermute | solution.py:404
  16.6 24.8 %collective-permute-start.2 = (f32[2,256,256]{2,1,0:T(8,128)S(1)}, f32[2,256,256]{2,1,0:T(8,128)S(1)}, u32[]{:S(2)}, u32[]{:S(2)}) collective-permute-start(f32[2,256,256]{2,1,0:T(8,128)S(1)} %get-tuple-element.25), channel_id=1, source_target_pairs={{0,3},{1,0},{2,1},{3,2},{4,7},{5,4},{6,5},{7,6},{8,11},{9,8},{10,9... | collective-permute-start | bytes 1572872 | tf_op jit(solution)/shard_map/ppermute | solution.py:404
  17.5 23.8 %collective-permute-start.3 = (f32[2,256,256]{2,1,0:T(8,128)S(1)}, f32[2,256,256]{2,1,0:T(8,128)S(1)}, u32[]{:S(2)}, u32[]{:S(2)}) collective-permute-start(f32[2,256,256]{2,1,0:T(8,128)S(1)} %get-tuple-element.22.refs_0_), channel_id=1, source_target_pairs={{12,28},{13,29},{14,30},{15,31},{28,12},{29,13},{30,14},{31,15},{4... | collective-permute-start | bytes 1572872 | tf_op jit(solution)/shard_map/ppermute | solution.py:404
  18.2 2.9 %collective-permute-start.5 = (f32[256,256]{1,0:T(8,128)S(1)}, f32[256,256]{1,0:T(8,128)S(1)}, u32[]{:S(2)}, u32[]{:S(2)}) collective-permute-start(f32[256,256]{1,0:T(8,128)S(1)} %collective-permute-done.4.direct), channel_id=1, source_target_pairs={{0,8},{1,9},{2,10},{3,11},{4,12},{5,13},{6,14},{7,15},{8,0},{9,1},... | collective-permute-start | bytes 786440 | tf_op jit(solution)/shard_map/ppermute | solution.py:404
  22.1 36.5 %copy-start.2 = (bf16[4,256,256]{2,1,0:T(8,128)(2,1)}, bf16[4,256,256]{2,1,0:T(8,128)(2,1)S(1)}, u32[]{:S(2)}) copy-start(bf16[4,256,256]{2,1,0:T(8,128)(2,1)S(1)} %get-tuple-element.27.refs_6_.all_refs_2_) | copy-start | bytes 1572868
  22.1 36.5 %copy-start.3 = (bf16[4,256,256]{2,1,0:T(8,128)(2,1)}, bf16[4,256,256]{2,1,0:T(8,128)(2,1)S(1)}, u32[]{:S(2)}) copy-start(bf16[4,256,256]{2,1,0:T(8,128)(2,1)S(1)} %get-tuple-element.28.refs_7_.all_refs_3_) | copy-start | bytes 1572868
  22.2 36.5 %copy-start.4 = (bf16[4,256,256]{2,1,0:T(8,128)(2,1)}, bf16[4,256,256]{2,1,0:T(8,128)(2,1)S(1)}, u32[]{:S(2)}) copy-start(bf16[4,256,256]{2,1,0:T(8,128)(2,1)S(1)} %get-tuple-element.29.refs_8_.all_refs_4_) | copy-start | bytes 1572868
  22.2 36.5 %copy-start.5 = (bf16[4,256,256]{2,1,0:T(8,128)(2,1)}, bf16[4,256,256]{2,1,0:T(8,128)(2,1)S(1)}, u32[]{:S(2)}) copy-start(bf16[4,256,256]{2,1,0:T(8,128)(2,1)S(1)} %get-tuple-element.30.refs_9_.all_refs_5_) | copy-start | bytes 1572868
  51.2 7.7 %copy-start.10 = (f32[4,2,256,256]{3,2,1,0:T(8,128)}, f32[4,2,256,256]{3,2,1,0:T(8,128)S(1)}, u32[]{:S(2)}) copy-start(f32[4,2,256,256]{3,2,1,0:T(8,128)S(1)} %get-tuple-element.31.all_refs_0_) | copy-start | bytes 6291460
  51.2 7.4 %collective-permute-start.8 = (f32[2,256,256]{2,1,0:T(8,128)S(1)}, f32[2,256,256]{2,1,0:T(8,128)S(1)}, u32[]{:S(2)}, u32[]{:S(2)}) collective-permute-start(f32[2,256,256]{2,1,0:T(8,128)S(1)} %get-tuple-element.32), channel_id=1, source_target_pairs={{0,4},{1,5},{2,6},{3,7},{8,28},{9,29},{10,30},{11,31},{16,20},{17,... | collective-permute-start | bytes 1572872 | tf_op jit(solution)/shard_map/ppermute | solution.py:404
  58.9 27.7 %collective-permute-start.9 = (f32[2,256,256]{2,1,0:T(8,128)S(1)}, f32[2,256,256]{2,1,0:T(8,128)S(1)}, u32[]{:S(2)}, u32[]{:S(2)}) collective-permute-start(f32[2,256,256]{2,1,0:T(8,128)S(1)} %get-tuple-element.33), channel_id=1, source_target_pairs={{4,0},{5,1},{6,2},{7,3},{28,8},{29,9},{30,10},{31,11},{20,16},{21,... | collective-permute-start | bytes 1572872 | tf_op jit(solution)/shard_map/ppermute | solution.py:404
  86.6 52.7 %copy-start.6 = (f32[1,256,256]{2,1,0:T(8,128)S(1)}, f32[1,256,256]{2,1,0:T(8,128)}, u32[]{:S(2)}) copy-start(f32[1,256,256]{2,1,0:T(8,128)} %refs_2_.1) | copy-start | bytes 786436
  86.6 52.7 %copy-start.7 = (s32[1,256]{1,0:T(1,128)S(1)}, s32[1,256]{1,0:T(1,128)}, u32[]{:S(2)}) copy-start(s32[1,256]{1,0:T(1,128)} %refs_3_.1) | copy-start | bytes 3076
  86.6 52.7 %copy-start.8 = (f32[3]{0:T(128)S(1)}, f32[3]{0:T(128)}, u32[]{:S(2)}) copy-start(f32[3]{0:T(128)} %refs_0_.1) | copy-start | bytes 40
  86.6 52.7 %copy-start.9 = (s32[3]{0:T(128)S(1)}, s32[3]{0:T(128)}, u32[]{:S(2)}) copy-start(s32[3]{0:T(128)} %refs_1_.1) | copy-start | bytes 40
  94.4 4.4 %collective-permute-start.10 = (f32[2,256,256]{2,1,0:T(8,128)S(1)}, f32[2,256,256]{2,1,0:T(8,128)S(1)}, u32[]{:S(2)}, u32[]{:S(2)}) collective-permute-start(f32[2,256,256]{2,1,0:T(8,128)S(1)} %get-tuple-element.38), channel_id=1, source_target_pairs={{0,0},{1,1},{2,2},{3,3},{4,4},{5,5},{6,6},{7,7},{8,8},{9,9},{10,10... | collective-permute-start | bytes 1572872 | tf_op jit(solution)/shard_map/ppermute | solution.py:404
  95.1 13.8 %collective-permute-start.11 = (f32[2,256,256]{2,1,0:T(8,128)S(1)}, f32[2,256,256]{2,1,0:T(8,128)S(1)}, u32[]{:S(2)}, u32[]{:S(2)}) collective-permute-start(f32[2,256,256]{2,1,0:T(8,128)S(1)} %get-tuple-element.39), channel_id=1, source_target_pairs={{0,1},{1,2},{2,3},{3,0},{4,5},{5,6},{6,7},{7,4},{8,9},{9,10},{10,1... | collective-permute-start | bytes 1572872 | tf_op jit(solution)/shard_map/ppermute | solution.py:404
  95.6 25.3 %collective-permute-start.12 = (f32[2,256,256]{2,1,0:T(8,128)S(1)}, f32[2,256,256]{2,1,0:T(8,128)S(1)}, u32[]{:S(2)}, u32[]{:S(2)}) collective-permute-start(f32[2,256,256]{2,1,0:T(8,128)S(1)} %get-tuple-element.40), channel_id=1, source_target_pairs={{0,2},{1,3},{2,0},{3,1},{4,6},{5,7},{6,4},{7,5},{8,10},{9,11},{10,... | collective-permute-start | bytes 1572872 | tf_op jit(solution)/shard_map/ppermute | solution.py:404
  98.7 28.6 %collective-permute-start.13 = (f32[2,256,256]{2,1,0:T(8,128)S(1)}, f32[2,256,256]{2,1,0:T(8,128)S(1)}, u32[]{:S(2)}, u32[]{:S(2)}) collective-permute-start(f32[2,256,256]{2,1,0:T(8,128)S(1)} %get-tuple-element.41), channel_id=1, source_target_pairs={{0,3},{1,0},{2,1},{3,2},{4,7},{5,4},{6,5},{7,6},{8,11},{9,8},{10,9... | collective-permute-start | bytes 1572872 | tf_op jit(solution)/shard_map/ppermute | solution.py:404
  98.7 30.5 %collective-permute-start.14 = (f32[2,256,256]{2,1,0:T(8,128)S(1)}, f32[2,256,256]{2,1,0:T(8,128)S(1)}, u32[]{:S(2)}, u32[]{:S(2)}) collective-permute-start(f32[2,256,256]{2,1,0:T(8,128)S(1)} %collective-permute-done.10.refs_4_), channel_id=1, source_target_pairs={{2,10},{3,11},{6,14},{7,15},{8,0},{9,1},{10,18},{11,19},{12,4},{13... | collective-permute-start | bytes 1572872 | tf_op jit(solution)/shard_map/ppermute | solution.py:404
  108.9 20.3 %collective-permute-start.15 = (f32[2,256,256]{2,1,0:T(8,128)S(1)}, f32[2,256,256]{2,1,0:T(8,128)S(1)}, u32[]{:S(2)}, u32[]{:S(2)}) collective-permute-start(f32[2,256,256]{2,1,0:T(8,128)S(1)} %collective-permute-done.11.refs_5_), channel_id=1, source_target_pairs={{0,8},{3,11},{4,12},{7,15},{8,16},{9,1},{10,2},{11,19},{12,20},{13... | collective-permute-start | bytes 1572872 | tf_op jit(solution)/shard_map/ppermute | solution.py:404
  120.9 18.1 %collective-permute-start.16 = (f32[2,256,256]{2,1,0:T(8,128)S(1)}, f32[2,256,256]{2,1,0:T(8,128)S(1)}, u32[]{:S(2)}, u32[]{:S(2)}) collective-permute-start(f32[2,256,256]{2,1,0:T(8,128)S(1)} %collective-permute-done.12.refs_6_), channel_id=1, source_target_pairs={{0,8},{1,9},{4,12},{5,13},{8,16},{9,17},{10,2},{11,3},{12,20},{13,... | collective-permute-start | bytes 1572872 | tf_op jit(solution)/shard_map/ppermute | solution.py:404
  127.3 12.0 %collective-permute-start.17 = (f32[2,256,256]{2,1,0:T(8,128)S(1)}, f32[2,256,256]{2,1,0:T(8,128)S(1)}, u32[]{:S(2)}, u32[]{:S(2)}) collective-permute-start(f32[2,256,256]{2,1,0:T(8,128)S(1)} %collective-permute-done.13.refs_7_), channel_id=1, source_target_pairs={{1,9},{2,10},{5,13},{6,14},{8,0},{9,17},{10,18},{11,3},{12,4},{13,... | collective-permute-start | bytes 1572872 | tf_op jit(solution)/shard_map/ppermute | solution.py:404
where the time goes:
time: 145 us; the launch traced here: 144 us
  waiting for transfers between devices  76.6 us (53%)
  starting transfers between devices  39.7 us (27%)
  Pallas kernels  24.6 us (17%)
  local copies, waits for them, and re-layouts  1.69 us (1%)
    ppermute x18, waiting for transfers between devices, send(): return lax.ppermute(value, AXES, pairs)  76.6 us
    ppermute x18, starting transfers between devices, send(): return lax.ppermute(value, AXES, pairs)  39.7 us
    pallas_call x6, Pallas kernels, run(): return pl.pallas_call(kernel, **options)(*operands)  24.6 us
  transfers between devices with their start and end apart: 18, of which 11 were waited for; matrix products, arithmetic and copies ran while one was open for 0% of the time, Pallas kernels for 2%

commit v1 on v0

--- a/solution.py
+++ b/solution.py
@@ -356,13 +356,38 @@
 def scatter_kernel(*refs):
     strength_ref, offsets_ref, coupling_ref, groups_ref = refs[:4]
     blocks, halos = refs[4 : 4 + X], refs[4 + X : 4 + 2 * X]
-    green_ref, self_ref = refs[4 + 2 * X : 6 + 2 * X]
-    own, side, out, in_sems, out_sems = refs[6 + 2 * X :]
-    x, _, _ = place()
-    for turn in range(X):
+    moved, risen = refs[4 + 2 * X], refs[4 + 2 * X : 4 + 3 * X]
+    green_ref, self_ref = refs[4 + 3 * X : 6 + 3 * X]
+    own, side, out, in_sems, out_sems = refs[6 + 3 * X :]
+    x, z, core = place()
+
+    def fetch(block, target, row, turn):
         index = lax.rem(x - turn + X, X)
-        pltpu.make_async_copy(blocks[turn], own.at[index], in_sems.at[index]).start()
-        pltpu.make_async_copy(halos[turn], side.at[index], in_sems.at[X + index]).start()
+        pltpu.make_async_copy(block, target.at[index], in_sems.at[row * X + index]).start()
+
+    away = (z == 1) & (core == 1)
+
+    @pl.when(away)
+    def _():
+        fetch(moved, own, 0, 0)
+
+    @pl.when(jnp.logical_not(away))
+    def _():
+        fetch(blocks[0], own, 0, 0)
+
+    for turn in range(1, X):
+        fetch(blocks[turn], own, 0, turn)
+    fetch(halos[0], side, 1, 0)
+    for turn in range(1, X):
+        above = (z == 1) & (core == 0) & (lax.rem(x - turn + X, X) >= 2)
+
+        @pl.when(above)
+        def _(turn=turn):
+            fetch(risen[turn], side, 1, turn)
+
+        @pl.when(jnp.logical_not(above))
+        def _(turn=turn):
+            fetch(halos[turn], side, 1, turn)
 
     weights = []
     for distance in (1, 2):
@@ -376,17 +401,23 @@
     matrix = jnp.where(groups == groups.T, coupling_ref[0], 0.0)
     left, right = split(matrix), split(matrix.T)
     store = []
-    for index in range(X):
+
+    def arrive(index):
         pltpu.make_async_copy(blocks[0], own.at[index], in_sems.at[index]).wait()
         copy = pltpu.make_async_copy(own.at[index], green_ref.at[index, 0], out_sems.at[index])
         copy.start()
         store.append(copy)
-    for index in range(X):
+
+    def arrive_aside(index):
         pltpu.make_async_copy(blocks[0], side.at[index], in_sems.at[X + index]).wait()
 
     def energy(index):
         return side[index + X] if index < 0 else own[index] if index < X else side[index - X]
 
+    for index in range(X):
+        arrive(index)
+    for index in range(X):
+        arrive_aside(index)
     for index in range(X):
         near = energy(index - 1) + energy(index + 1)
         far = energy(index - 2) + energy(index + 2)
@@ -458,23 +489,28 @@
             pairs = []
             for c in chunks:
                 for s in lanes:
-                    if turn or back or host(c, s) != c:
+                    if turn or host(c, s) != c:
                         ends = (host(c, s), c) if back else (c, host(c, s))
                         pairs.append((device(ends[0], s), device(ends[1], shifted(s, turn))))
             result.append(send(values[turn], pairs))
         return result
 
-    def halo(values):
-        result = []
-        for turn in range(X):
-            pairs = []
-            for c in chunks:
-                for s in lanes:
-                    target = c - 1 if (s - turn) % X < 2 else c + 1
-                    if 0 <= target < count:
-                        pairs.append((device(c, s), device(target, s)))
-            result.append(send(values[turn], pairs))
-        return result
+    def halo(value, turn):
+        pairs = []
+        for c in chunks:
+            for s in lanes:
+                target = c - 1 if (s - turn) % X < 2 else c + 1
+                near = turn and s >= X and c % 2 and target > c
+                if 0 <= target < count and not near:
+                    pairs.append((device(c if turn else host(c, s), s), device(target, s)))
+        return send(value, pairs)
+
+    def rise(value, turn):
+        pairs = []
+        for c in chunks[1:-1:2]:
+            for s in range(X + 2, 2 * X):
+                pairs.append((device(host(c, s), s), device(c + 1, shifted(s, turn))))
+        return send(value, pairs)
 
     up = [(device(c, s), device(host(c, s + X), s + X)) for c in chunks for s in range(X)]
     down = [(target, source) for source, target in up]
@@ -484,8 +520,10 @@
     *greens, message = second("middle", lined_up, message, parts)
     message = send(message, down)
     greens = second("last", lined_up, message, parts, greens)
-    greens = exchange(greens, True)
-    halos = halo(greens)
+    own, hosted = greens[0], greens
+    moved, *greens = exchange(greens, True)
+    halos = [halo(own if turn == 0 else greens[turn - 1], turn) for turn in range(X)]
+    risen = [rise(hosted[turn], turn) for turn in range(1, X)]
 
     return call(
         scatter_kernel,
@@ -493,7 +531,7 @@
             jax.ShapeDtypeStruct((X, 1, 2, W, W), F32),
             jax.ShapeDtypeStruct((X, 1, 2, W, W), F32),
         ),
-        in_specs=[SMEM, SMEM, VMEM, VMEM] + [ANY] * (2 * X),
+        in_specs=[SMEM, SMEM, VMEM, VMEM] + [ANY] * (3 * X),
         out_specs=[ANY, ANY],
         scratch_shapes=[
             pltpu.VMEM((X, 2, W, W), F32),
@@ -505,7 +543,7 @@
         name="scatter",
         compiler_params=pltpu.CompilerParams(vmem_limit_bytes=LIMIT),
         cost_estimate=cost(16),
-    )(strength, offsets, coupling, groups, *greens, *halos)
+    )(strength, offsets, coupling, groups, own, *greens, *halos, moved, *risen)
 
 
 def solution(mesh):

time: 145 us -> 154 us (1.062)
  the two profiles are of different devices: /device:TPU:1 before, /device:TPU:49 now
where the time goes in v1:
time: 154 us; the launch traced here: 153 us
  waiting for transfers between devices  71.6 us (46%)
  starting transfers between devices  54.3 us (35%)
  Pallas kernels  24.5 us (16%)
  local copies, waits for them, and re-layouts  1.69 us (1%)
    ppermute x21, waiting for transfers between devices, send(): return lax.ppermute(value, AXES, pairs)  71.6 us
    ppermute x21, starting transfers between devices, send(): return lax.ppermute(value, AXES, pairs)  54.3 us
    pallas_call x6, Pallas kernels, run(): return pl.pallas_call(kernel, **options)(*operands)  24.5 us
  transfers between devices with their start and end apart: 21, of which 13 were waited for; matrix products, arithmetic and copies ran while one was open for 0% of the time, Pallas kernels for 2%

profile of v1, /device:TPU:49, one launch (start us, length us, event | category | flops | bytes accessed | tf_op | source)
XLA Modules:
  0.0 153.1 jit_solution(3757743598882351569)
XLA Ops:
  1.6 2.8 %collective-permute-start.6 = (f32[128,256]{1,0:T(8,128)S(1)}, f32[128,256]{1,0:T(8,128)S(1)}, u32[]{:S(2)}, u32[]{:S(2)}) collective-permute-start(f32[128,256]{1,0:T(8,128)S(1)} %dynamic-slice_bitcast_fusion), channel_id=1, source_target_pairs={{0,2},{1,3},{2,0},{3,1},{4,6},{5,7},{6,4},{7,5},{8,10},{9,11},{10,... | collective-permute-start | bytes 393224 | tf_op jit(solution)/shard_map/ppermute | solution.py:435
  4.4 3.1 %collective-permute-done.6.half = f32[128,256]{1,0:T(8,128)S(1)} collective-permute-done((f32[128,256]{1,0:T(8,128)S(1)}, f32[128,256]{1,0:T(8,128)S(1)}, u32[]{:S(2)}, u32[]{:S(2)}) %collective-permute-start.6) | collective-permute-done | bytes 131104 | tf_op jit(solution)/shard_map/ppermute | solution.py:435
  7.6 1.5 collective-permute-start.7
  9.1 2.5 %collective-permute-start.4 = (f32[256,256]{1,0:T(8,128)}, f32[256,256]{1,0:T(8,128)S(1)}, u32[]{:S(2)}, u32[]{:S(2)}) collective-permute-start(f32[256,256]{1,0:T(8,128)} %bitcast.4), channel_id=1, source_target_pairs={{0,1},{1,2},{2,3},{3,0},{4,5},{5,6},{6,7},{7,4},{8,11},{9,8},{10,9... | collective-permute-start | bytes 786440 | tf_op jit(solution)/shard_map/ppermute | solution.py:435
  12.3 1.7 %systems.1 = (f32[2,256,256]{2,1,0:T(8,128)S(1)}, f32[2,256,256]{2,1,0:T(8,128)S(1)}, f32[2,256,256]{2,1,0:T(8,128)S(1)}, f32[2,256,256]{2,1,0:T(8,128)S(1)}) custom-call(f32[4,1,2,256,256]{4,3,2,1,0:T(8,128)} %self_ref.1, f32[1,256]{1,0:T(1,128)S(1)} %copy-done.2, f32[1,256,256]{2,1,0:T(8,128)} %within_ref.1, s32[1]{0:T(128)} %bitcast.first_ref), custom_call_target="tpu_custom_call" | custom-call | tf_op jit(solution)/shard_map/systems/pallas_call | solution.py:309
  14.0 1.5 collective-permute-start
  15.4 2.7 %collective-permute-start.1 = (f32[2,256,256]{2,1,0:T(8,128)S(1)}, f32[2,256,256]{2,1,0:T(8,128)S(1)}, u32[]{:S(2)}, u32[]{:S(2)}) collective-permute-start(f32[2,256,256]{2,1,0:T(8,128)S(1)} %get-tuple-element.24), channel_id=1, source_target_pairs={{0,2},{1,3},{2,0},{3,1},{4,6},{5,7},{6,4},{7,5},{8,10},{9,11},{10,... | collective-permute-start | bytes 1572872 | tf_op jit(solution)/shard_map/ppermute | solution.py:435
  18.2 3.3 %collective-permute-start.2 = (f32[2,256,256]{2,1,0:T(8,128)S(1)}, f32[2,256,256]{2,1,0:T(8,128)S(1)}, u32[]{:S(2)}, u32[]{:S(2)}) collective-permute-start(f32[2,256,256]{2,1,0:T(8,128)S(1)} %get-tuple-element.25), channel_id=1, source_target_pairs={{0,3},{1,0},{2,1},{3,2},{4,7},{5,4},{6,5},{7,6},{8,11},{9,8},{10,9... | collective-permute-start | bytes 1572872 | tf_op jit(solution)/shard_map/ppermute | solution.py:435
  21.5 2.3 %collective-permute-start.3 = (f32[2,256,256]{2,1,0:T(8,128)S(1)}, f32[2,256,256]{2,1,0:T(8,128)S(1)}, u32[]{:S(2)}, u32[]{:S(2)}) collective-permute-start(f32[2,256,256]{2,1,0:T(8,128)S(1)} %get-tuple-element.22.refs_0_), channel_id=1, source_target_pairs={{12,28},{13,29},{14,30},{15,31},{28,12},{29,13},{30,14},{31,15},{4... | collective-permute-start | bytes 1572872 | tf_op jit(solution)/shard_map/ppermute | solution.py:435
  23.8 1.5 collective-permute-done.5.swapped
  26.3 5.0 %collective-permute-done.refs_1_ = f32[2,256,256]{2,1,0:T(8,128)S(1)} collective-permute-done((f32[2,256,256]{2,1,0:T(8,128)S(1)}, f32[2,256,256]{2,1,0:T(8,128)S(1)}, u32[]{:S(2)}, u32[]{:S(2)}) %collective-permute-start) | collective-permute-done | bytes 524320 | tf_op jit(solution)/shard_map/ppermute | solution.py:435
  31.3 10.9 %collective-permute-done.1.refs_2_ = f32[2,256,256]{2,1,0:T(8,128)S(1)} collective-permute-done((f32[2,256,256]{2,1,0:T(8,128)S(1)}, f32[2,256,256]{2,1,0:T(8,128)S(1)}, u32[]{:S(2)}, u32[]{:S(2)}) %collective-permute-start.1) | collective-permute-done | bytes 524320 | tf_op jit(solution)/shard_map/ppermute | solution.py:435
  42.2 1.4 collective-permute-done.2.refs_3_
  43.6 2.5 %collective-permute-done.3.refs_4_ = f32[2,256,256]{2,1,0:T(8,128)S(1)} collective-permute-done((f32[2,256,256]{2,1,0:T(8,128)S(1)}, f32[2,256,256]{2,1,0:T(8,128)S(1)}, u32[]{:S(2)}, u32[]{:S(2)}) %collective-permute-start.3) | collective-permute-done | bytes 524320 | tf_op jit(solution)/shard_map/ppermute | solution.py:435
  46.4 1.3 collective-permute-start.8
  47.7 12.3 %collective-permute-done.8.all_refs_1_ = f32[2,256,256]{2,1,0:T(8,128)S(1)} collective-permute-done((f32[2,256,256]{2,1,0:T(8,128)S(1)}, f32[2,256,256]{2,1,0:T(8,128)S(1)}, u32[]{:S(2)}, u32[]{:S(2)}) %collective-permute-start.8) | collective-permute-done | bytes 524320 | tf_op jit(solution)/shard_map/ppermute | solution.py:435
  60.0 17.1 %recursion_middle.1 = (f32[2,256,256]{2,1,0:T(8,128)S(1)}, f32[2,256,256]{2,1,0:T(8,128)S(1)}, f32[2,256,256]{2,1,0:T(8,128)S(1)}, f32[2,256,256]{2,1,0:T(8,128)S(1)}, f32[2,256,256]{2,1,0:T(8,128)S(1)}) custom-call(f32[4,2,256,256]{3,2,1,0:T(8,128)S(1)} %get-tuple-element.31.all_refs_0_, f32[2,256,256]{2,1,0:T(8,128)S(1)} %collective-permute-done.8.all_refs_1_, ...), custom_call_target="tpu_custom_call" | custom-call | flops 10468982784 | bytes 6291456 | tf_op jit(solution)/shard_map/recursion_middle/pallas_call | solution.py:309
  77.1 1.3 collective-permute-start.9
  78.4 6.1 %collective-permute-done.9.all_refs_1_ = f32[2,256,256]{2,1,0:T(8,128)S(1)} collective-permute-done((f32[2,256,256]{2,1,0:T(8,128)S(1)}, f32[2,256,256]{2,1,0:T(8,128)S(1)}, u32[]{:S(2)}, u32[]{:S(2)}) %collective-permute-start.9) | collective-permute-done | bytes 524320 | tf_op jit(solution)/shard_map/ppermute | solution.py:435
  86.5 8.7 %collective-permute-start.11 = (f32[2,256,256]{2,1,0:T(8,128)S(1)}, f32[2,256,256]{2,1,0:T(8,128)S(1)}, u32[]{:S(2)}, u32[]{:S(2)}) collective-permute-start(f32[2,256,256]{2,1,0:T(8,128)S(1)} %get-tuple-element.40), channel_id=1, source_target_pairs={{0,2},{1,3},{2,0},{3,1},{4,6},{5,7},{6,4},{7,5},{8,10},{9,11},{10,... | collective-permute-start | bytes 1572872 | tf_op jit(solution)/shard_map/ppermute | solution.py:435
  95.9 7.9 %collective-permute-start.12 = (f32[2,256,256]{2,1,0:T(8,128)S(1)}, f32[2,256,256]{2,1,0:T(8,128)S(1)}, u32[]{:S(2)}, u32[]{:S(2)}) collective-permute-start(f32[2,256,256]{2,1,0:T(8,128)S(1)} %get-tuple-element.41), channel_id=1, source_target_pairs={{0,3},{1,0},{2,1},{3,2},{4,7},{5,4},{6,5},{7,6},{8,11},{9,8},{10,9... | collective-permute-start | bytes 1572872 | tf_op jit(solution)/shard_map/ppermute | solution.py:435
  103.8 11.1 %collective-permute-done.10.refs_5_ = f32[2,256,256]{2,1,0:T(8,128)S(1)} collective-permute-done((f32[2,256,256]{2,1,0:T(8,128)S(1)}, f32[2,256,256]{2,1,0:T(8,128)S(1)}, u32[]{:S(2)}, u32[]{:S(2)}) %collective-permute-start.10) | collective-permute-done | bytes 524320 | tf_op jit(solution)/shard_map/ppermute | solution.py:435
  114.9 2.8 %collective-permute-start.17 = (f32[2,256,256]{2,1,0:T(8,128)S(1)}, f32[2,256,256]{2,1,0:T(8,128)S(1)}, u32[]{:S(2)}, u32[]{:S(2)}) collective-permute-start(f32[2,256,256]{2,1,0:T(8,128)S(1)} %get-tuple-element.38.refs_4_), channel_id=1, source_target_pairs={{28,12},{29,13},{30,14},{31,15},{12,28},{13,29},{14,30},{15,31},{6... | collective-permute-start | bytes 1572872 | tf_op jit(solution)/shard_map/ppermute | solution.py:435
  117.7 7.6 %collective-permute-start.13 = (f32[2,256,256]{2,1,0:T(8,128)S(1)}, f32[2,256,256]{2,1,0:T(8,128)S(1)}, u32[]{:S(2)}, u32[]{:S(2)}) collective-permute-start(f32[2,256,256]{2,1,0:T(8,128)S(1)} %get-tuple-element.38.refs_4_), channel_id=1, source_target_pairs={{2,10},{3,11},{6,14},{7,15},{8,0},{9,1},{10,18},{11,19},{28,4},{29... | collective-permute-start | bytes 1572872 | tf_op jit(solution)/shard_map/ppermute | solution.py:435
  125.3 3.0 %collective-permute-done.11.refs_6_ = f32[2,256,256]{2,1,0:T(8,128)S(1)} collective-permute-done((f32[2,256,256]{2,1,0:T(8,128)S(1)}, f32[2,256,256]{2,1,0:T(8,128)S(1)}, u32[]{:S(2)}, u32[]{:S(2)}) %collective-permute-start.11) | collective-permute-done | bytes 524320 | tf_op jit(solution)/shard_map/ppermute | solution.py:435
  128.3 1.3 collective-permute-start.14
  129.6 1.3 collective-permute-start.15
  130.9 3.1 %collective-permute-start.16 = (f32[2,256,256]{2,1,0:T(8,128)S(1)}, f32[2,256,256]{2,1,0:T(8,128)S(1)}, u32[]{:S(2)}, u32[]{:S(2)}) collective-permute-start(f32[2,256,256]{2,1,0:T(8,128)S(1)} %collective-permute-done.12.refs_7_), channel_id=1, source_target_pairs={{1,9},{2,10},{5,13},{6,14},{8,0},{9,17},{10,18},{11,3},{12,4},{15,... | collective-permute-start | bytes 1572872 | tf_op jit(solution)/shard_map/ppermute | solution.py:435
  134.0 1.5 collective-permute-done.17.refs_12_
  135.5 10.8 %collective-permute-done.13.refs_8_ = f32[2,256,256]{2,1,0:T(8,128)S(1)} collective-permute-done((f32[2,256,256]{2,1,0:T(8,128)S(1)}, f32[2,256,256]{2,1,0:T(8,128)S(1)}, u32[]{:S(2)}, u32[]{:S(2)}) %collective-permute-start.13) | collective-permute-done | bytes 524320 | tf_op jit(solution)/shard_map/ppermute | solution.py:435
  146.3 2.5 %collective-permute-done.16.refs_11_ = f32[2,256,256]{2,1,0:T(8,128)S(1)} collective-permute-done((f32[2,256,256]{2,1,0:T(8,128)S(1)}, f32[2,256,256]{2,1,0:T(8,128)S(1)}, u32[]{:S(2)}, u32[]{:S(2)}) %collective-permute-start.16) | collective-permute-done | bytes 524320 | tf_op jit(solution)/shard_map/ppermute | solution.py:435
  148.8 4.2 %scatter.1 = (f32[4,1,2,256,256]{4,3,2,1,0:T(8,128)}, f32[4,1,2,256,256]{4,3,2,1,0:T(8,128)}) custom-call(f32[3]{0:T(128)S(1)} %copy-done.4, s32[3]{0:T(128)S(1)} %copy-done.5, f32[1,256,256]{2,1,0:T(8,128)S(1)} %copy-done.1, s32[1,256]{1,0:T(1,128)S(1)} %copy-done.3, f32[2,256,256]{2,1,0:T(8,128)S(1)} %get-tuple-element.38.refs_4_, ...), custom_call_target="tpu_custom_call" | custom-call | flops 1610612736 | bytes 6291456 | tf_op jit(solution)/shard_map/scatter/pallas_call | solution.py:309
  (39 shorter events, 5.6 us)
Async XLA Ops:
  0.6 24.7 %copy-start = (f32[1,256,256]{2,1,0:T(8,128)S(1)}, f32[1,256,256]{2,1,0:T(8,128)}, u32[]{:S(2)}) copy-start(f32[1,256,256]{2,1,0:T(8,128)} %own.1) | copy-start | bytes 786436
  1.6 6.0 %collective-permute-start.6 = (f32[128,256]{1,0:T(8,128)S(1)}, f32[128,256]{1,0:T(8,128)S(1)}, u32[]{:S(2)}, u32[]{:S(2)}) collective-permute-start(f32[128,256]{1,0:T(8,128)S(1)} %dynamic-slice_bitcast_fusion), channel_id=1, source_target_pairs={{0,2},{1,3},{2,0},{3,1},{4,6},{5,7},{6,4},{7,5},{8,10},{9,11},{10,... | collective-permute-start | bytes 393224 | tf_op jit(solution)/shard_map/ppermute | solution.py:435
  7.6 13.9 %collective-permute-start.7 = (f32[128,256]{1,0:T(8,128)S(1)}, f32[128,256]{1,0:T(8,128)S(1)}, u32[]{:S(2)}, u32[]{:S(2)}) collective-permute-start(f32[128,256]{1,0:T(8,128)S(1)} %collective-permute-done.6.half), channel_id=1, source_target_pairs={{0,8},{1,9},{2,10},{3,11},{4,12},{5,13},{6,14},{7,15},{8,0},{9,1},... | collective-permute-start | bytes 393224 | tf_op jit(solution)/shard_map/ppermute | solution.py:435
  9.1 14.6 %collective-permute-start.4 = (f32[256,256]{1,0:T(8,128)}, f32[256,256]{1,0:T(8,128)S(1)}, u32[]{:S(2)}, u32[]{:S(2)}) collective-permute-start(f32[256,256]{1,0:T(8,128)} %bitcast.4), channel_id=1, source_target_pairs={{0,1},{1,2},{2,3},{3,0},{4,5},{5,6},{6,7},{7,4},{8,11},{9,8},{10,9... | collective-permute-start | bytes 786440 | tf_op jit(solution)/shard_map/ppermute | solution.py:435
  11.6 0.7 copy-start.2
  14.0 17.3 %collective-permute-start = (f32[2,256,256]{2,1,0:T(8,128)S(1)}, f32[2,256,256]{2,1,0:T(8,128)S(1)}, u32[]{:S(2)}, u32[]{:S(2)}) collective-permute-start(f32[2,256,256]{2,1,0:T(8,128)S(1)} %get-tuple-element.23), channel_id=1, source_target_pairs={{0,1},{1,2},{2,3},{3,0},{4,5},{5,6},{6,7},{7,4},{8,9},{9,10},{10,1... | collective-permute-start | bytes 1572872 | tf_op jit(solution)/shard_map/ppermute | solution.py:435
  15.4 26.7 %collective-permute-start.1 = (f32[2,256,256]{2,1,0:T(8,128)S(1)}, f32[2,256,256]{2,1,0:T(8,128)S(1)}, u32[]{:S(2)}, u32[]{:S(2)}) collective-permute-start(f32[2,256,256]{2,1,0:T(8,128)S(1)} %get-tuple-element.24), channel_id=1, source_target_pairs={{0,2},{1,3},{2,0},{3,1},{4,6},{5,7},{6,4},{7,5},{8,10},{9,11},{10,... | collective-permute-start | bytes 1572872 | tf_op jit(solution)/shard_map/ppermute | solution.py:435
  18.2 25.4 %collective-permute-start.2 = (f32[2,256,256]{2,1,0:T(8,128)S(1)}, f32[2,256,256]{2,1,0:T(8,128)S(1)}, u32[]{:S(2)}, u32[]{:S(2)}) collective-permute-start(f32[2,256,256]{2,1,0:T(8,128)S(1)} %get-tuple-element.25), channel_id=1, source_target_pairs={{0,3},{1,0},{2,1},{3,2},{4,7},{5,4},{6,5},{7,6},{8,11},{9,8},{10,9... | collective-permute-start | bytes 1572872 | tf_op jit(solution)/shard_map/ppermute | solution.py:435
  21.5 24.7 %collective-permute-start.3 = (f32[2,256,256]{2,1,0:T(8,128)S(1)}, f32[2,256,256]{2,1,0:T(8,128)S(1)}, u32[]{:S(2)}, u32[]{:S(2)}) collective-permute-start(f32[2,256,256]{2,1,0:T(8,128)S(1)} %get-tuple-element.22.refs_0_), channel_id=1, source_target_pairs={{12,28},{13,29},{14,30},{15,31},{28,12},{29,13},{30,14},{31,15},{4... | collective-permute-start | bytes 1572872 | tf_op jit(solution)/shard_map/ppermute | solution.py:435
  23.7 1.6 %collective-permute-start.5 = (f32[256,256]{1,0:T(8,128)S(1)}, f32[256,256]{1,0:T(8,128)S(1)}, u32[]{:S(2)}, u32[]{:S(2)}) collective-permute-start(f32[256,256]{1,0:T(8,128)S(1)} %collective-permute-done.4.direct), channel_id=1, source_target_pairs={{0,8},{1,9},{2,10},{3,11},{4,12},{5,13},{6,14},{7,15},{8,0},{9,1},... | collective-permute-start | bytes 786440 | tf_op jit(solution)/shard_map/ppermute | solution.py:435
  26.3 33.7 %copy-start.6 = (bf16[4,256,256]{2,1,0:T(8,128)(2,1)}, bf16[4,256,256]{2,1,0:T(8,128)(2,1)S(1)}, u32[]{:S(2)}) copy-start(bf16[4,256,256]{2,1,0:T(8,128)(2,1)S(1)} %get-tuple-element.27.refs_6_.all_refs_2_) | copy-start | bytes 1572868
  26.3 33.6 %copy-start.7 = (bf16[4,256,256]{2,1,0:T(8,128)(2,1)}, bf16[4,256,256]{2,1,0:T(8,128)(2,1)S(1)}, u32[]{:S(2)}) copy-start(bf16[4,256,256]{2,1,0:T(8,128)(2,1)S(1)} %get-tuple-element.28.refs_7_.all_refs_3_) | copy-start | bytes 1572868
  26.3 33.6 %copy-start.8 = (bf16[4,256,256]{2,1,0:T(8,128)(2,1)}, bf16[4,256,256]{2,1,0:T(8,128)(2,1)S(1)}, u32[]{:S(2)}) copy-start(bf16[4,256,256]{2,1,0:T(8,128)(2,1)S(1)} %get-tuple-element.29.refs_8_.all_refs_4_) | copy-start | bytes 1572868
  26.3 33.6 %copy-start.9 = (bf16[4,256,256]{2,1,0:T(8,128)(2,1)}, bf16[4,256,256]{2,1,0:T(8,128)(2,1)S(1)}, u32[]{:S(2)}) copy-start(bf16[4,256,256]{2,1,0:T(8,128)(2,1)S(1)} %get-tuple-element.30.refs_9_.all_refs_5_) | copy-start | bytes 1572868
  46.3 30.7 %copy-start.10 = (f32[4,2,256,256]{3,2,1,0:T(8,128)}, f32[4,2,256,256]{3,2,1,0:T(8,128)S(1)}, u32[]{:S(2)}) copy-start(f32[4,2,256,256]{3,2,1,0:T(8,128)S(1)} %get-tuple-element.31.all_refs_0_) | copy-start | bytes 6291460
  46.4 13.6 %collective-permute-start.8 = (f32[2,256,256]{2,1,0:T(8,128)S(1)}, f32[2,256,256]{2,1,0:T(8,128)S(1)}, u32[]{:S(2)}, u32[]{:S(2)}) collective-permute-start(f32[2,256,256]{2,1,0:T(8,128)S(1)} %get-tuple-element.32), channel_id=1, source_target_pairs={{0,4},{1,5},{2,6},{3,7},{8,28},{9,29},{10,30},{11,31},{16,20},{17,... | collective-permute-start | bytes 1572872 | tf_op jit(solution)/shard_map/ppermute | solution.py:435
  77.1 7.4 %collective-permute-start.9 = (f32[2,256,256]{2,1,0:T(8,128)S(1)}, f32[2,256,256]{2,1,0:T(8,128)S(1)}, u32[]{:S(2)}, u32[]{:S(2)}) collective-permute-start(f32[2,256,256]{2,1,0:T(8,128)S(1)} %get-tuple-element.33), channel_id=1, source_target_pairs={{4,0},{5,1},{6,2},{7,3},{28,8},{29,9},{30,10},{31,11},{20,16},{21,... | collective-permute-start | bytes 1572872 | tf_op jit(solution)/shard_map/ppermute | solution.py:435
  84.5 64.3 %copy-start.1 = (f32[1,256,256]{2,1,0:T(8,128)S(1)}, f32[1,256,256]{2,1,0:T(8,128)}, u32[]{:S(2)}) copy-start(f32[1,256,256]{2,1,0:T(8,128)} %refs_2_.1) | copy-start | bytes 786436
  84.5 64.3 %copy-start.3 = (s32[1,256]{1,0:T(1,128)S(1)}, s32[1,256]{1,0:T(1,128)}, u32[]{:S(2)}) copy-start(s32[1,256]{1,0:T(1,128)} %refs_3_.1) | copy-start | bytes 3076
  84.5 64.3 %copy-start.4 = (f32[3]{0:T(128)S(1)}, f32[3]{0:T(128)}, u32[]{:S(2)}) copy-start(f32[3]{0:T(128)} %refs_0_.1) | copy-start | bytes 40
  84.5 64.3 %copy-start.5 = (s32[3]{0:T(128)S(1)}, s32[3]{0:T(128)}, u32[]{:S(2)}) copy-start(s32[3]{0:T(128)} %refs_1_.1) | copy-start | bytes 40
  84.9 11.0 %collective-permute-start.18 = (f32[2,256,256]{2,1,0:T(8,128)S(1)}, f32[2,256,256]{2,1,0:T(8,128)S(1)}, u32[]{:S(2)}, u32[]{:S(2)}) collective-permute-start(f32[2,256,256]{2,1,0:T(8,128)S(1)} %get-tuple-element.39), channel_id=1, source_target_pairs={{30,23},{31,20},{14,39},{15,36},{62,55},{63,52},{46,71},{47,68},{9... | collective-permute-start | bytes 1572872 | tf_op jit(solution)/shard_map/ppermute | solution.py:435
  85.6 29.3 %collective-permute-start.10 = (f32[2,256,256]{2,1,0:T(8,128)S(1)}, f32[2,256,256]{2,1,0:T(8,128)S(1)}, u32[]{:S(2)}, u32[]{:S(2)}) collective-permute-start(f32[2,256,256]{2,1,0:T(8,128)S(1)} %get-tuple-element.39), channel_id=1, source_target_pairs={{0,1},{1,2},{2,3},{3,0},{4,5},{5,6},{6,7},{7,4},{8,9},{9,10},{10,1... | collective-permute-start | bytes 1572872 | tf_op jit(solution)/shard_map/ppermute | solution.py:435
  85.8 31.9 %collective-permute-start.19 = (f32[2,256,256]{2,1,0:T(8,128)S(1)}, f32[2,256,256]{2,1,0:T(8,128)S(1)}, u32[]{:S(2)}, u32[]{:S(2)}) collective-permute-start(f32[2,256,256]{2,1,0:T(8,128)S(1)} %get-tuple-element.40), channel_id=1, source_target_pairs={{30,20},{31,21},{14,36},{15,37},{62,52},{63,53},{46,68},{47,69},{9... | collective-permute-start | bytes 1572872 | tf_op jit(solution)/shard_map/ppermute | solution.py:435
  86.5 41.8 %collective-permute-start.11 = (f32[2,256,256]{2,1,0:T(8,128)S(1)}, f32[2,256,256]{2,1,0:T(8,128)S(1)}, u32[]{:S(2)}, u32[]{:S(2)}) collective-permute-start(f32[2,256,256]{2,1,0:T(8,128)S(1)} %get-tuple-element.40), channel_id=1, source_target_pairs={{0,2},{1,3},{2,0},{3,1},{4,6},{5,7},{6,4},{7,5},{8,10},{9,11},{10,... | collective-permute-start | bytes 1572872 | tf_op jit(solution)/shard_map/ppermute | solution.py:435
  95.2 34.4 %collective-permute-start.20 = (f32[2,256,256]{2,1,0:T(8,128)S(1)}, f32[2,256,256]{2,1,0:T(8,128)S(1)}, u32[]{:S(2)}, u32[]{:S(2)}) collective-permute-start(f32[2,256,256]{2,1,0:T(8,128)S(1)} %get-tuple-element.41), channel_id=1, source_target_pairs={{30,21},{31,22},{14,37},{15,38},{62,53},{63,54},{46,69},{47,70},{9... | collective-permute-start | bytes 1572872 | tf_op jit(solution)/shard_map/ppermute | solution.py:435
  95.9 35.0 %collective-permute-start.12 = (f32[2,256,256]{2,1,0:T(8,128)S(1)}, f32[2,256,256]{2,1,0:T(8,128)S(1)}, u32[]{:S(2)}, u32[]{:S(2)}) collective-permute-start(f32[2,256,256]{2,1,0:T(8,128)S(1)} %get-tuple-element.41), channel_id=1, source_target_pairs={{0,3},{1,0},{2,1},{3,2},{4,7},{5,4},{6,5},{7,6},{8,11},{9,8},{10,9... | collective-permute-start | bytes 1572872 | tf_op jit(solution)/shard_map/ppermute | solution.py:435
  114.9 20.6 %collective-permute-start.17 = (f32[2,256,256]{2,1,0:T(8,128)S(1)}, f32[2,256,256]{2,1,0:T(8,128)S(1)}, u32[]{:S(2)}, u32[]{:S(2)}) collective-permute-start(f32[2,256,256]{2,1,0:T(8,128)S(1)} %get-tuple-element.38.refs_4_), channel_id=1, source_target_pairs={{28,12},{29,13},{30,14},{31,15},{12,28},{13,29},{14,30},{15,31},{6... | collective-permute-start | bytes 1572872 | tf_op jit(solution)/shard_map/ppermute | solution.py:435
  117.7 28.6 %collective-permute-start.13 = (f32[2,256,256]{2,1,0:T(8,128)S(1)}, f32[2,256,256]{2,1,0:T(8,128)S(1)}, u32[]{:S(2)}, u32[]{:S(2)}) collective-permute-start(f32[2,256,256]{2,1,0:T(8,128)S(1)} %get-tuple-element.38.refs_4_), channel_id=1, source_target_pairs={{2,10},{3,11},{6,14},{7,15},{8,0},{9,1},{10,18},{11,19},{28,4},{29... | collective-permute-start | bytes 1572872 | tf_op jit(solution)/shard_map/ppermute | solution.py:435
  128.3 18.0 %collective-permute-start.14 = (f32[2,256,256]{2,1,0:T(8,128)S(1)}, f32[2,256,256]{2,1,0:T(8,128)S(1)}, u32[]{:S(2)}, u32[]{:S(2)}) collective-permute-start(f32[2,256,256]{2,1,0:T(8,128)S(1)} %collective-permute-done.10.refs_5_), channel_id=1, source_target_pairs={{0,8},{3,11},{4,12},{7,15},{8,16},{9,1},{10,2},{11,19},{13,5},{14,... | collective-permute-start | bytes 1572872 | tf_op jit(solution)/shard_map/ppermute | solution.py:435
  129.6 16.7 %collective-permute-start.15 = (f32[2,256,256]{2,1,0:T(8,128)S(1)}, f32[2,256,256]{2,1,0:T(8,128)S(1)}, u32[]{:S(2)}, u32[]{:S(2)}) collective-permute-start(f32[2,256,256]{2,1,0:T(8,128)S(1)} %collective-permute-done.11.refs_6_), channel_id=1, source_target_pairs={{0,8},{1,9},{4,12},{5,13},{8,16},{9,17},{10,2},{11,3},{14,6},{15,7... | collective-permute-start | bytes 1572872 | tf_op jit(solution)/shard_map/ppermute | solution.py:435
  130.9 17.8 %collective-permute-start.16 = (f32[2,256,256]{2,1,0:T(8,128)S(1)}, f32[2,256,256]{2,1,0:T(8,128)S(1)}, u32[]{:S(2)}, u32[]{:S(2)}) collective-permute-start(f32[2,256,256]{2,1,0:T(8,128)S(1)} %collective-permute-done.12.refs_7_), channel_id=1, source_target_pairs={{1,9},{2,10},{5,13},{6,14},{8,0},{9,17},{10,18},{11,3},{12,4},{15,... | collective-permute-start | bytes 1572872 | tf_op jit(solution)/shard_map/ppermute | solution.py:435

commit v2 on v1

--- a/solution.py
+++ b/solution.py
@@ -353,41 +353,65 @@
     )(blocks, message, *parts, *after)
 
 
-def scatter_kernel(*refs):
-    strength_ref, offsets_ref, coupling_ref, groups_ref = refs[:4]
-    blocks, halos = refs[4 : 4 + X], refs[4 + X : 4 + 2 * X]
-    moved, risen = refs[4 + 2 * X], refs[4 + 2 * X : 4 + 3 * X]
-    green_ref, self_ref = refs[4 + 3 * X : 6 + 3 * X]
-    own, side, out, in_sems, out_sems = refs[6 + 3 * X :]
+def gather_kernel(*refs):
+    coupling_ref, groups_ref, blocks, moved = refs[0], refs[1], refs[2 : 2 + X], refs[2 + X]
+    green_ref, own = refs[3 + X], refs[4 + X]
+    matrices, in_sems, out_sems = refs[5 + X : 9 + X], refs[9 + X], refs[10 + X]
     x, z, core = place()
 
-    def fetch(block, target, row, turn):
+    def fetch(block, turn):
         index = lax.rem(x - turn + X, X)
-        pltpu.make_async_copy(block, target.at[index], in_sems.at[row * X + index]).start()
+        pltpu.make_async_copy(block, own.at[index], in_sems.at[index]).start()
 
     away = (z == 1) & (core == 1)
 
     @pl.when(away)
     def _():
-        fetch(moved, own, 0, 0)
+        fetch(moved, 0)
 
     @pl.when(jnp.logical_not(away))
     def _():
-        fetch(blocks[0], own, 0, 0)
+        fetch(blocks[0], 0)
 
     for turn in range(1, X):
-        fetch(blocks[turn], own, 0, turn)
-    fetch(halos[0], side, 1, 0)
+        fetch(blocks[turn], turn)
+    groups = jnp.broadcast_to(groups_ref[...], (W, W)).astype(F32)
+    matrix = jnp.where(groups == groups.T, coupling_ref[0], 0.0)
+    matrices[0][...], matrices[1][...] = split(matrix)
+    matrices[2][...], matrices[3][...] = split(matrix.T)
+    store = []
+    for index in range(X):
+        pltpu.make_async_copy(blocks[0], own.at[index], in_sems.at[index]).wait()
+        store.append(
+            pltpu.make_async_copy(own.at[index], green_ref.at[index, 0], out_sems.at[index])
+        )
+        store[-1].start()
+    for copy in store:
+        copy.wait()
+
+
+def scatter_kernel(*refs):
+    strength_ref, offsets_ref, own, matrices = refs[0], refs[1], refs[2], refs[3:7]
+    halos = refs[7 : 7 + X]
+    self_ref, side, out, in_sems, out_sems = refs[6 + 2 * X :]
+    risen = (None, *refs[7 + X : 6 + 2 * X])
+    x, z, core = place()
+
+    def fetch(block, turn):
+        index = lax.rem(x - turn + X, X)
+        pltpu.make_async_copy(block, side.at[index], in_sems.at[index]).start()
+
+    fetch(halos[0], 0)
     for turn in range(1, X):
         above = (z == 1) & (core == 0) & (lax.rem(x - turn + X, X) >= 2)
 
         @pl.when(above)
         def _(turn=turn):
-            fetch(risen[turn], side, 1, turn)
+            fetch(risen[turn], turn)
 
         @pl.when(jnp.logical_not(above))
         def _(turn=turn):
-            fetch(halos[turn], side, 1, turn)
+            fetch(halos[turn], turn)
 
     weights = []
     for distance in (1, 2):
@@ -397,34 +421,22 @@
                 for mode in range(MODES)
             )
         )
-    groups = jnp.broadcast_to(groups_ref[...], (W, W)).astype(F32)
-    matrix = jnp.where(groups == groups.T, coupling_ref[0], 0.0)
-    left, right = split(matrix), split(matrix.T)
+    left = matrices[0][...], matrices[1][...]
+    right = matrices[2][...], matrices[3][...]
     store = []
-
-    def arrive(index):
-        pltpu.make_async_copy(blocks[0], own.at[index], in_sems.at[index]).wait()
-        copy = pltpu.make_async_copy(own.at[index], green_ref.at[index, 0], out_sems.at[index])
-        copy.start()
-        store.append(copy)
-
-    def arrive_aside(index):
-        pltpu.make_async_copy(blocks[0], side.at[index], in_sems.at[X + index]).wait()
+    for index in range(X):
+        pltpu.make_async_copy(halos[0], side.at[index], in_sems.at[index]).wait()
 
     def energy(index):
         return side[index + X] if index < 0 else own[index] if index < X else side[index - X]
 
-    for index in range(X):
-        arrive(index)
-    for index in range(X):
-        arrive_aside(index)
     for index in range(X):
         near = energy(index - 1) + energy(index + 1)
         far = energy(index - 2) + energy(index + 2)
         total = weights[0] * near + weights[1] * far
         for part in range(2):
             out[index, part] = between_hops(left, total[part], right)
-        copy = pltpu.make_async_copy(out.at[index], self_ref.at[index, 0], out_sems.at[X + index])
+        copy = pltpu.make_async_copy(out.at[index], self_ref.at[index, 0], out_sems.at[index])
         copy.start()
         store.append(copy)
     for copy in store:
@@ -525,25 +537,33 @@
     halos = [halo(own if turn == 0 else greens[turn - 1], turn) for turn in range(X)]
     risen = [rise(hosted[turn], turn) for turn in range(1, X)]
 
-    return call(
+    green, own, *matrices = call(
+        gather_kernel,
+        out_shape=(jax.ShapeDtypeStruct((X, 1, 2, W, W), F32), SLABS4)
+        + (jax.ShapeDtypeStruct((W, W), BF16),) * 4,
+        in_specs=[VMEM, VMEM] + [ANY] * (X + 1),
+        out_specs=[ANY] + [VMEM] * 5,
+        scratch_shapes=[pltpu.SemaphoreType.DMA((X,)), pltpu.SemaphoreType.DMA((X,))],
+        name="gather",
+        compiler_params=pltpu.CompilerParams(vmem_limit_bytes=LIMIT),
+        cost_estimate=cost(2),
+    )(coupling, groups, own, *greens, moved)
+    self_out = call(
         scatter_kernel,
-        out_shape=(
-            jax.ShapeDtypeStruct((X, 1, 2, W, W), F32),
-            jax.ShapeDtypeStruct((X, 1, 2, W, W), F32),
-        ),
-        in_specs=[SMEM, SMEM, VMEM, VMEM] + [ANY] * (3 * X),
-        out_specs=[ANY, ANY],
+        out_shape=jax.ShapeDtypeStruct((X, 1, 2, W, W), F32),
+        in_specs=[SMEM, SMEM] + [VMEM] * 5 + [ANY] * (2 * X - 1),
+        out_specs=ANY,
         scratch_shapes=[
             pltpu.VMEM((X, 2, W, W), F32),
             pltpu.VMEM((X, 2, W, W), F32),
-            pltpu.VMEM((X, 2, W, W), F32),
-            pltpu.SemaphoreType.DMA((2 * X,)),
-            pltpu.SemaphoreType.DMA((2 * X,)),
+            pltpu.SemaphoreType.DMA((X,)),
+            pltpu.SemaphoreType.DMA((X,)),
         ],
         name="scatter",
         compiler_params=pltpu.CompilerParams(vmem_limit_bytes=LIMIT),
         cost_estimate=cost(16),
-    )(strength, offsets, coupling, groups, own, *greens, *halos, moved, *risen)
+    )(strength, offsets, own, *matrices, *halos, *risen)
+    return green, self_out
 
 
 def solution(mesh):

time: 154 us -> 144 us (0.935)
  the two profiles are of different devices: /device:TPU:49 before, /device:TPU:1 now
where the time goes in v2:
time: 144 us; the launch traced here: 143 us
  waiting for transfers between devices  77 us (53%)
  starting transfers between devices  37.1 us (26%)
  Pallas kernels  26.2 us (18%)
  local copies, waits for them, and re-layouts  1.67 us (1%)
    ppermute x21, waiting for transfers between devices, send(): return lax.ppermute(value, AXES, pairs)  77 us
    ppermute x21, starting transfers between devices, send(): return lax.ppermute(value, AXES, pairs)  37.1 us
    pallas_call x7, Pallas kernels, run(): return pl.pallas_call(kernel, **options)(*operands)  26.2 us
  transfers between devices with their start and end apart: 21, of which 9 were waited for; matrix products, arithmetic and copies ran while one was open for 1% of the time, Pallas kernels for 3%

profile of v2, /device:TPU:1, one launch (start us, length us, event | category | flops | bytes accessed | tf_op | source)
XLA Modules:
  0.0 143.0 jit_solution(12683360457460209501)
XLA Ops:
  0.6 3.4 %collective-permute-start.4 = (f32[256,256]{1,0:T(8,128)}, f32[256,256]{1,0:T(8,128)S(1)}, u32[]{:S(2)}, u32[]{:S(2)}) collective-permute-start(f32[256,256]{1,0:T(8,128)} %bitcast.4), channel_id=1, source_target_pairs={{0,1},{1,2},{2,3},{3,0},{4,5},{5,6},{6,7},{7,4},{8,11},{9,8},{10,9... | collective-permute-start | bytes 786440 | tf_op jit(solution)/shard_map/ppermute | solution.py:447
  4.0 0.9 dynamic-slice_bitcast_fusion
  6.2 1.7 %systems.1 = (f32[2,256,256]{2,1,0:T(8,128)S(1)}, f32[2,256,256]{2,1,0:T(8,128)S(1)}, f32[2,256,256]{2,1,0:T(8,128)S(1)}, f32[2,256,256]{2,1,0:T(8,128)S(1)}) custom-call(f32[4,1,2,256,256]{4,3,2,1,0:T(8,128)} %self_ref.1, f32[1,256]{1,0:T(1,128)S(1)} %copy-done.2, f32[1,256,256]{2,1,0:T(8,128)} %within_ref.1, s32[1]{0:T(128)} %bitcast.first_ref), custom_call_target="tpu_custom_call" | custom-call | tf_op jit(solution)/shard_map/systems/pallas_call | solution.py:309
  8.6 1.9 %collective-permute-start.1 = (f32[2,256,256]{2,1,0:T(8,128)S(1)}, f32[2,256,256]{2,1,0:T(8,128)S(1)}, u32[]{:S(2)}, u32[]{:S(2)}) collective-permute-start(f32[2,256,256]{2,1,0:T(8,128)S(1)} %get-tuple-element.30), channel_id=1, source_target_pairs={{0,2},{1,3},{2,0},{3,1},{4,6},{5,7},{6,4},{7,5},{8,10},{9,11},{10,... | collective-permute-start | bytes 1572872 | tf_op jit(solution)/shard_map/ppermute | solution.py:447
  10.5 2.0 %collective-permute-start.2 = (f32[2,256,256]{2,1,0:T(8,128)S(1)}, f32[2,256,256]{2,1,0:T(8,128)S(1)}, u32[]{:S(2)}, u32[]{:S(2)}) collective-permute-start(f32[2,256,256]{2,1,0:T(8,128)S(1)} %get-tuple-element.31), channel_id=1, source_target_pairs={{0,3},{1,0},{2,1},{3,2},{4,7},{5,4},{6,5},{7,6},{8,11},{9,8},{10,9... | collective-permute-start | bytes 1572872 | tf_op jit(solution)/shard_map/ppermute | solution.py:447
  12.5 0.7 collective-permute-start.3
  13.2 2.7 %collective-permute-start.7 = (f32[128,256]{1,0:T(8,128)S(1)}, f32[128,256]{1,0:T(8,128)S(1)}, u32[]{:S(2)}, u32[]{:S(2)}) collective-permute-start(f32[128,256]{1,0:T(8,128)S(1)} %collective-permute-done.6.half), channel_id=1, source_target_pairs={{0,8},{1,9},{2,10},{3,11},{4,12},{5,13},{6,14},{7,15},{8,0},{9,1},... | collective-permute-start | bytes 393224 | tf_op jit(solution)/shard_map/ppermute | solution.py:447
  15.9 1.0 collective-permute-done.7.other
  17.3 1.2 collective-permute-done.5.swapped
  18.4 0.9 prepare.1
  19.4 4.3 %collective-permute-done.refs_1_ = f32[2,256,256]{2,1,0:T(8,128)S(1)} collective-permute-done((f32[2,256,256]{2,1,0:T(8,128)S(1)}, f32[2,256,256]{2,1,0:T(8,128)S(1)}, u32[]{:S(2)}, u32[]{:S(2)}) %collective-permute-start) | collective-permute-done | bytes 524320 | tf_op jit(solution)/shard_map/ppermute | solution.py:447
  23.7 10.8 %collective-permute-done.1.refs_2_ = f32[2,256,256]{2,1,0:T(8,128)S(1)} collective-permute-done((f32[2,256,256]{2,1,0:T(8,128)S(1)}, f32[2,256,256]{2,1,0:T(8,128)S(1)}, u32[]{:S(2)}, u32[]{:S(2)}) %collective-permute-start.1) | collective-permute-done | bytes 524320 | tf_op jit(solution)/shard_map/ppermute | solution.py:447
  34.5 9.9 %recursion_first.1 = (f32[4,2,256,256]{3,2,1,0:T(8,128)S(1)}, f32[2,256,256]{2,1,0:T(8,128)S(1)}) custom-call(f32[2,256,256]{2,1,0:T(8,128)S(1)} %get-tuple-element.28.refs_0_, f32[2,256,256]{2,1,0:T(8,128)S(1)} %collective-permute-done.refs_1_, f32[2,256,256]{2,1,0:T(8,128)S(1)} %collective-permute-done.1.refs_2_, ...), custom_call_target="tpu_custom_call" | custom-call | flops 6442450944 | bytes 6291456 | tf_op jit(solution)/shard_map/recursion_first/pallas_call | solution.py:309
  44.5 1.3 collective-permute-start.8
  45.8 6.1 %collective-permute-done.8.all_refs_1_ = f32[2,256,256]{2,1,0:T(8,128)S(1)} collective-permute-done((f32[2,256,256]{2,1,0:T(8,128)S(1)}, f32[2,256,256]{2,1,0:T(8,128)S(1)}, u32[]{:S(2)}, u32[]{:S(2)}) %collective-permute-start.8) | collective-permute-done | bytes 524320 | tf_op jit(solution)/shard_map/ppermute | solution.py:447
  52.1 1.3 collective-permute-start.9
  53.4 26.4 %collective-permute-done.9.all_refs_1_ = f32[2,256,256]{2,1,0:T(8,128)S(1)} collective-permute-done((f32[2,256,256]{2,1,0:T(8,128)S(1)}, f32[2,256,256]{2,1,0:T(8,128)S(1)}, u32[]{:S(2)}, u32[]{:S(2)}) %collective-permute-start.9) | collective-permute-done | bytes 524320 | tf_op jit(solution)/shard_map/ppermute | solution.py:447
  79.9 7.7 %recursion_last.1 = (f32[2,256,256]{2,1,0:T(8,128)S(1)}, f32[2,256,256]{2,1,0:T(8,128)S(1)}, f32[2,256,256]{2,1,0:T(8,128)S(1)}, f32[2,256,256]{2,1,0:T(8,128)S(1)}) custom-call(f32[4,2,256,256]{3,2,1,0:T(8,128)} %copy-done.10, f32[2,256,256]{2,1,0:T(8,128)S(1)} %collective-permute-done.9.all_refs_1_, bf16[4,256,256]{2,1,0:T(8,128)(2,1)} %copy-done.6, ...), custom_call_target="tpu_custom_call" | custom-call | flops 4026531840 | bytes 6291456 | tf_op jit(solution)/shard_map/recursion_last/pallas_call | solution.py:309
  87.6 1.5 %collective-permute-start.10 = (f32[2,256,256]{2,1,0:T(8,128)S(1)}, f32[2,256,256]{2,1,0:T(8,128)S(1)}, u32[]{:S(2)}, u32[]{:S(2)}) collective-permute-start(f32[2,256,256]{2,1,0:T(8,128)S(1)} %get-tuple-element.45), channel_id=1, source_target_pairs={{0,1},{1,2},{2,3},{3,0},{4,5},{5,6},{6,7},{7,4},{8,9},{9,10},{10,1... | collective-permute-start | bytes 1572872 | tf_op jit(solution)/shard_map/ppermute | solution.py:447
  89.1 2.5 %collective-permute-start.11 = (f32[2,256,256]{2,1,0:T(8,128)S(1)}, f32[2,256,256]{2,1,0:T(8,128)S(1)}, u32[]{:S(2)}, u32[]{:S(2)}) collective-permute-start(f32[2,256,256]{2,1,0:T(8,128)S(1)} %get-tuple-element.46), channel_id=1, source_target_pairs={{0,2},{1,3},{2,0},{3,1},{4,6},{5,7},{6,4},{7,5},{8,10},{9,11},{10,... | collective-permute-start | bytes 1572872 | tf_op jit(solution)/shard_map/ppermute | solution.py:447
  92.7 4.4 %collective-permute-start.14 = (f32[2,256,256]{2,1,0:T(8,128)S(1)}, f32[2,256,256]{2,1,0:T(8,128)S(1)}, u32[]{:S(2)}, u32[]{:S(2)}) collective-permute-start(f32[2,256,256]{2,1,0:T(8,128)S(1)} %get-tuple-element.44.refs_2_), channel_id=1, source_target_pairs={{2,10},{3,11},{6,14},{7,15},{8,0},{9,1},{10,18},{11,19},{28,4},{29... | collective-permute-start | bytes 1572872 | tf_op jit(solution)/shard_map/ppermute | solution.py:447
  97.1 3.1 %collective-permute-done.10.refs_3_ = f32[2,256,256]{2,1,0:T(8,128)S(1)} collective-permute-done((f32[2,256,256]{2,1,0:T(8,128)S(1)}, f32[2,256,256]{2,1,0:T(8,128)S(1)}, u32[]{:S(2)}, u32[]{:S(2)}) %collective-permute-start.10) | collective-permute-done | bytes 524320 | tf_op jit(solution)/shard_map/ppermute | solution.py:447
  100.2 0.7 collective-permute-start.18
  100.9 12.9 %collective-permute-done.11.refs_4_ = f32[2,256,256]{2,1,0:T(8,128)S(1)} collective-permute-done((f32[2,256,256]{2,1,0:T(8,128)S(1)}, f32[2,256,256]{2,1,0:T(8,128)S(1)}, u32[]{:S(2)}, u32[]{:S(2)}) %collective-permute-start.11) | collective-permute-done | bytes 524320 | tf_op jit(solution)/shard_map/ppermute | solution.py:447
  113.8 0.7 collective-permute-start.19
  114.5 0.7 collective-permute-start.20
  115.2 6.4 %collective-permute-start.15 = (f32[2,256,256]{2,1,0:T(8,128)S(1)}, f32[2,256,256]{2,1,0:T(8,128)S(1)}, u32[]{:S(2)}, u32[]{:S(2)}) collective-permute-start(f32[2,256,256]{2,1,0:T(8,128)S(1)} %collective-permute-done.10.refs_3_), channel_id=1, source_target_pairs={{0,8},{3,11},{4,12},{7,15},{8,16},{9,1},{10,2},{11,19},{13,5},{14,... | collective-permute-start | bytes 1572872 | tf_op jit(solution)/shard_map/ppermute | solution.py:447
  121.6 1.9 %collective-permute-start.16 = (f32[2,256,256]{2,1,0:T(8,128)S(1)}, f32[2,256,256]{2,1,0:T(8,128)S(1)}, u32[]{:S(2)}, u32[]{:S(2)}) collective-permute-start(f32[2,256,256]{2,1,0:T(8,128)S(1)} %collective-permute-done.11.refs_4_), channel_id=1, source_target_pairs={{0,8},{1,9},{4,12},{5,13},{8,16},{9,17},{10,2},{11,3},{14,6},{15,7... | collective-permute-start | bytes 1572872 | tf_op jit(solution)/shard_map/ppermute | solution.py:447
  123.5 2.4 %collective-permute-start.17 = (f32[2,256,256]{2,1,0:T(8,128)S(1)}, f32[2,256,256]{2,1,0:T(8,128)S(1)}, u32[]{:S(2)}, u32[]{:S(2)}) collective-permute-start(f32[2,256,256]{2,1,0:T(8,128)S(1)} %collective-permute-done.12.refs_5_), channel_id=1, source_target_pairs={{1,9},{2,10},{5,13},{6,14},{8,0},{9,17},{10,18},{11,3},{12,4},{15,... | collective-permute-start | bytes 1572872 | tf_op jit(solution)/shard_map/ppermute | solution.py:447
  126.0 1.8 %gather.1 = (f32[4,1,2,256,256]{4,3,2,1,0:T(8,128)}, f32[4,2,256,256]{3,2,1,0:T(8,128)S(1)}, bf16[256,256]{1,0:T(8,128)(2,1)S(1)}, bf16[256,256]{1,0:T(8,128)(2,...) custom-call(f32[1,256,256]{2,1,0:T(8,128)S(1)} %copy-done.1, s32[1,256]{1,0:T(1,128)S(1)} %copy-done.3, ...), custom_call_target="tpu_custom_call" | custom-call | flops 201326592 | bytes 6291456 | tf_op jit(solution)/shard_map/gather/pallas_call | solution.py:309
  127.8 11.1 %collective-permute-done.16.refs_9_ = f32[2,256,256]{2,1,0:T(8,128)S(1)} collective-permute-done((f32[2,256,256]{2,1,0:T(8,128)S(1)}, f32[2,256,256]{2,1,0:T(8,128)S(1)}, u32[]{:S(2)}, u32[]{:S(2)}) %collective-permute-start.16) | collective-permute-done | bytes 524320 | tf_op jit(solution)/shard_map/ppermute | solution.py:447
  138.9 3.9 %scatter.1 = f32[4,1,2,256,256]{4,3,2,1,0:T(8,128)} custom-call(f32[3]{0:T(128)S(1)} %copy-done.4, s32[3]{0:T(128)S(1)} %copy-done.5, f32[4,2,256,256]{3,2,1,0:T(8,128)S(1)} %get-tuple-element.49.refs_2_, bf16[256,256]{1,0:T(8,128)(2,1)S(1)} %get-tuple-element.50.refs_3_, bf16[256,256]{1,0:T(8,128)(2,1)S(1)} %get-tuple-element.51.refs_4_, ...), custom_call_target="tpu_custom_call" | custom-call | flops 1610612736 | bytes 6291456 | tf_op jit(solution)/shard_map/scatter/pallas_call | solution.py:309
  (40 shorter events, 3.7 us)
Async XLA Ops:
  0.6 17.8 %copy-start = (f32[1,256,256]{2,1,0:T(8,128)S(1)}, f32[1,256,256]{2,1,0:T(8,128)}, u32[]{:S(2)}) copy-start(f32[1,256,256]{2,1,0:T(8,128)} %own.1) | copy-start | bytes 786436
  0.6 12.6 %collective-permute-start.4 = (f32[256,256]{1,0:T(8,128)}, f32[256,256]{1,0:T(8,128)S(1)}, u32[]{:S(2)}, u32[]{:S(2)}) collective-permute-start(f32[256,256]{1,0:T(8,128)} %bitcast.4), channel_id=1, source_target_pairs={{0,1},{1,2},{2,3},{3,0},{4,5},{5,6},{6,7},{7,4},{8,11},{9,8},{10,9... | collective-permute-start | bytes 786440 | tf_op jit(solution)/shard_map/ppermute | solution.py:447
  5.0 7.6 %collective-permute-start.6 = (f32[128,256]{1,0:T(8,128)S(1)}, f32[128,256]{1,0:T(8,128)S(1)}, u32[]{:S(2)}, u32[]{:S(2)}) collective-permute-start(f32[128,256]{1,0:T(8,128)S(1)} %dynamic-slice_bitcast_fusion), channel_id=1, source_target_pairs={{0,2},{1,3},{2,0},{3,1},{4,6},{5,7},{6,4},{7,5},{8,10},{9,11},{10,... | collective-permute-start | bytes 393224 | tf_op jit(solution)/shard_map/ppermute | solution.py:447
  5.6 0.7 copy-start.2
  7.9 15.8 %collective-permute-start = (f32[2,256,256]{2,1,0:T(8,128)S(1)}, f32[2,256,256]{2,1,0:T(8,128)S(1)}, u32[]{:S(2)}, u32[]{:S(2)}) collective-permute-start(f32[2,256,256]{2,1,0:T(8,128)S(1)} %get-tuple-element.29), channel_id=1, source_target_pairs={{0,1},{1,2},{2,3},{3,0},{4,5},{5,6},{6,7},{7,4},{8,9},{9,10},{10,1... | collective-permute-start | bytes 1572872 | tf_op jit(solution)/shard_map/ppermute | solution.py:447
  8.6 25.9 %collective-permute-start.1 = (f32[2,256,256]{2,1,0:T(8,128)S(1)}, f32[2,256,256]{2,1,0:T(8,128)S(1)}, u32[]{:S(2)}, u32[]{:S(2)}) collective-permute-start(f32[2,256,256]{2,1,0:T(8,128)S(1)} %get-tuple-element.30), channel_id=1, source_target_pairs={{0,2},{1,3},{2,0},{3,1},{4,6},{5,7},{6,4},{7,5},{8,10},{9,11},{10,... | collective-permute-start | bytes 1572872 | tf_op jit(solution)/shard_map/ppermute | solution.py:447
  10.5 24.0 %collective-permute-start.2 = (f32[2,256,256]{2,1,0:T(8,128)S(1)}, f32[2,256,256]{2,1,0:T(8,128)S(1)}, u32[]{:S(2)}, u32[]{:S(2)}) collective-permute-start(f32[2,256,256]{2,1,0:T(8,128)S(1)} %get-tuple-element.31), channel_id=1, source_target_pairs={{0,3},{1,0},{2,1},{3,2},{4,7},{5,4},{6,5},{7,6},{8,11},{9,8},{10,9... | collective-permute-start | bytes 1572872 | tf_op jit(solution)/shard_map/ppermute | solution.py:447
  12.5 22.0 %collective-permute-start.3 = (f32[2,256,256]{2,1,0:T(8,128)S(1)}, f32[2,256,256]{2,1,0:T(8,128)S(1)}, u32[]{:S(2)}, u32[]{:S(2)}) collective-permute-start(f32[2,256,256]{2,1,0:T(8,128)S(1)} %get-tuple-element.28.refs_0_), channel_id=1, source_target_pairs={{12,28},{13,29},{14,30},{15,31},{28,12},{29,13},{30,14},{31,15},{4... | collective-permute-start | bytes 1572872 | tf_op jit(solution)/shard_map/ppermute | solution.py:447
  13.2 3.7 %collective-permute-start.7 = (f32[128,256]{1,0:T(8,128)S(1)}, f32[128,256]{1,0:T(8,128)S(1)}, u32[]{:S(2)}, u32[]{:S(2)}) collective-permute-start(f32[128,256]{1,0:T(8,128)S(1)} %collective-permute-done.6.half), channel_id=1, source_target_pairs={{0,8},{1,9},{2,10},{3,11},{4,12},{5,13},{6,14},{7,15},{8,0},{9,1},... | collective-permute-start | bytes 393224 | tf_op jit(solution)/shard_map/ppermute | solution.py:447
  16.9 1.5 %collective-permute-start.5 = (f32[256,256]{1,0:T(8,128)S(1)}, f32[256,256]{1,0:T(8,128)S(1)}, u32[]{:S(2)}, u32[]{:S(2)}) collective-permute-start(f32[256,256]{1,0:T(8,128)S(1)} %collective-permute-done.4.direct), channel_id=1, source_target_pairs={{0,8},{1,9},{2,10},{3,11},{4,12},{5,13},{6,14},{7,15},{8,0},{9,1},... | collective-permute-start | bytes 786440 | tf_op jit(solution)/shard_map/ppermute | solution.py:447
  19.4 32.5 %copy-start.6 = (bf16[4,256,256]{2,1,0:T(8,128)(2,1)}, bf16[4,256,256]{2,1,0:T(8,128)(2,1)S(1)}, u32[]{:S(2)}) copy-start(bf16[4,256,256]{2,1,0:T(8,128)(2,1)S(1)} %get-tuple-element.33.refs_6_.all_refs_2_) | copy-start | bytes 1572868
  19.4 32.5 %copy-start.7 = (bf16[4,256,256]{2,1,0:T(8,128)(2,1)}, bf16[4,256,256]{2,1,0:T(8,128)(2,1)S(1)}, u32[]{:S(2)}) copy-start(bf16[4,256,256]{2,1,0:T(8,128)(2,1)S(1)} %get-tuple-element.34.refs_7_.all_refs_3_) | copy-start | bytes 1572868
  19.4 32.5 %copy-start.8 = (bf16[4,256,256]{2,1,0:T(8,128)(2,1)}, bf16[4,256,256]{2,1,0:T(8,128)(2,1)S(1)}, u32[]{:S(2)}) copy-start(bf16[4,256,256]{2,1,0:T(8,128)(2,1)S(1)} %get-tuple-element.35.refs_8_.all_refs_4_) | copy-start | bytes 1572868
  19.4 32.5 %copy-start.9 = (bf16[4,256,256]{2,1,0:T(8,128)(2,1)}, bf16[4,256,256]{2,1,0:T(8,128)(2,1)S(1)}, u32[]{:S(2)}) copy-start(bf16[4,256,256]{2,1,0:T(8,128)(2,1)S(1)} %get-tuple-element.36.refs_9_.all_refs_5_) | copy-start | bytes 1572868
  44.4 7.7 %copy-start.10 = (f32[4,2,256,256]{3,2,1,0:T(8,128)}, f32[4,2,256,256]{3,2,1,0:T(8,128)S(1)}, u32[]{:S(2)}) copy-start(f32[4,2,256,256]{3,2,1,0:T(8,128)S(1)} %get-tuple-element.37.all_refs_0_) | copy-start | bytes 6291460
  44.5 7.4 %collective-permute-start.8 = (f32[2,256,256]{2,1,0:T(8,128)S(1)}, f32[2,256,256]{2,1,0:T(8,128)S(1)}, u32[]{:S(2)}, u32[]{:S(2)}) collective-permute-start(f32[2,256,256]{2,1,0:T(8,128)S(1)} %get-tuple-element.38), channel_id=1, source_target_pairs={{0,4},{1,5},{2,6},{3,7},{8,28},{9,29},{10,30},{11,31},{16,20},{17,... | collective-permute-start | bytes 1572872 | tf_op jit(solution)/shard_map/ppermute | solution.py:447
  52.1 27.7 %collective-permute-start.9 = (f32[2,256,256]{2,1,0:T(8,128)S(1)}, f32[2,256,256]{2,1,0:T(8,128)S(1)}, u32[]{:S(2)}, u32[]{:S(2)}) collective-permute-start(f32[2,256,256]{2,1,0:T(8,128)S(1)} %get-tuple-element.39), channel_id=1, source_target_pairs={{4,0},{5,1},{6,2},{7,3},{28,8},{29,9},{30,10},{31,11},{20,16},{21,... | collective-permute-start | bytes 1572872 | tf_op jit(solution)/shard_map/ppermute | solution.py:447
  79.9 46.1 %copy-start.1 = (f32[1,256,256]{2,1,0:T(8,128)S(1)}, f32[1,256,256]{2,1,0:T(8,128)}, u32[]{:S(2)}) copy-start(f32[1,256,256]{2,1,0:T(8,128)} %refs_0_.2) | copy-start | bytes 786436
  79.9 46.1 %copy-start.3 = (s32[1,256]{1,0:T(1,128)S(1)}, s32[1,256]{1,0:T(1,128)}, u32[]{:S(2)}) copy-start(s32[1,256]{1,0:T(1,128)} %refs_1_.2) | copy-start | bytes 3076
  87.6 51.3 %copy-start.4 = (f32[3]{0:T(128)S(1)}, f32[3]{0:T(128)}, u32[]{:S(2)}) copy-start(f32[3]{0:T(128)} %refs_0_.3) | copy-start | bytes 40
  87.6 51.3 %copy-start.5 = (s32[3]{0:T(128)S(1)}, s32[3]{0:T(128)}, u32[]{:S(2)}) copy-start(s32[3]{0:T(128)} %refs_1_.3) | copy-start | bytes 40
  87.6 12.6 %collective-permute-start.10 = (f32[2,256,256]{2,1,0:T(8,128)S(1)}, f32[2,256,256]{2,1,0:T(8,128)S(1)}, u32[]{:S(2)}, u32[]{:S(2)}) collective-permute-start(f32[2,256,256]{2,1,0:T(8,128)S(1)} %get-tuple-element.45), channel_id=1, source_target_pairs={{0,1},{1,2},{2,3},{3,0},{4,5},{5,6},{6,7},{7,4},{8,9},{9,10},{10,1... | collective-permute-start | bytes 1572872 | tf_op jit(solution)/shard_map/ppermute | solution.py:447
  89.1 24.7 %collective-permute-start.11 = (f32[2,256,256]{2,1,0:T(8,128)S(1)}, f32[2,256,256]{2,1,0:T(8,128)S(1)}, u32[]{:S(2)}, u32[]{:S(2)}) collective-permute-start(f32[2,256,256]{2,1,0:T(8,128)S(1)} %get-tuple-element.46), channel_id=1, source_target_pairs={{0,2},{1,3},{2,0},{3,1},{4,6},{5,7},{6,4},{7,5},{8,10},{9,11},{10,... | collective-permute-start | bytes 1572872 | tf_op jit(solution)/shard_map/ppermute | solution.py:447
  91.6 22.9 %collective-permute-start.12 = (f32[2,256,256]{2,1,0:T(8,128)S(1)}, f32[2,256,256]{2,1,0:T(8,128)S(1)}, u32[]{:S(2)}, u32[]{:S(2)}) collective-permute-start(f32[2,256,256]{2,1,0:T(8,128)S(1)} %get-tuple-element.47), channel_id=1, source_target_pairs={{0,3},{1,0},{2,1},{3,2},{4,7},{5,4},{6,5},{7,6},{8,11},{9,8},{10,9... | collective-permute-start | bytes 1572872 | tf_op jit(solution)/shard_map/ppermute | solution.py:447
  92.0 23.2 %collective-permute-start.13 = (f32[2,256,256]{2,1,0:T(8,128)S(1)}, f32[2,256,256]{2,1,0:T(8,128)S(1)}, u32[]{:S(2)}, u32[]{:S(2)}) collective-permute-start(f32[2,256,256]{2,1,0:T(8,128)S(1)} %get-tuple-element.44.refs_2_), channel_id=1, source_target_pairs={{28,12},{29,13},{30,14},{31,15},{12,28},{13,29},{14,30},{15,31},{6... | collective-permute-start | bytes 1572872 | tf_op jit(solution)/shard_map/ppermute | solution.py:447
  92.7 28.9 %collective-permute-start.14 = (f32[2,256,256]{2,1,0:T(8,128)S(1)}, f32[2,256,256]{2,1,0:T(8,128)S(1)}, u32[]{:S(2)}, u32[]{:S(2)}) collective-permute-start(f32[2,256,256]{2,1,0:T(8,128)S(1)} %get-tuple-element.44.refs_2_), channel_id=1, source_target_pairs={{2,10},{3,11},{6,14},{7,15},{8,0},{9,1},{10,18},{11,19},{28,4},{29... | collective-permute-start | bytes 1572872 | tf_op jit(solution)/shard_map/ppermute | solution.py:447
  100.2 23.3 %collective-permute-start.18 = (f32[2,256,256]{2,1,0:T(8,128)S(1)}, f32[2,256,256]{2,1,0:T(8,128)S(1)}, u32[]{:S(2)}, u32[]{:S(2)}) collective-permute-start(f32[2,256,256]{2,1,0:T(8,128)S(1)} %get-tuple-element.45), channel_id=1, source_target_pairs={{30,23},{31,20},{14,39},{15,36},{62,55},{63,52},{46,71},{47,68},{9... | collective-permute-start | bytes 1572872 | tf_op jit(solution)/shard_map/ppermute | solution.py:447
  113.8 14.0 %collective-permute-start.19 = (f32[2,256,256]{2,1,0:T(8,128)S(1)}, f32[2,256,256]{2,1,0:T(8,128)S(1)}, u32[]{:S(2)}, u32[]{:S(2)}) collective-permute-start(f32[2,256,256]{2,1,0:T(8,128)S(1)} %get-tuple-element.46), channel_id=1, source_target_pairs={{30,20},{31,21},{14,36},{15,37},{62,52},{63,53},{46,68},{47,69},{9... | collective-permute-start | bytes 1572872 | tf_op jit(solution)/shard_map/ppermute | solution.py:447
  114.5 13.3 %collective-permute-start.20 = (f32[2,256,256]{2,1,0:T(8,128)S(1)}, f32[2,256,256]{2,1,0:T(8,128)S(1)}, u32[]{:S(2)}, u32[]{:S(2)}) collective-permute-start(f32[2,256,256]{2,1,0:T(8,128)S(1)} %get-tuple-element.47), channel_id=1, source_target_pairs={{30,21},{31,22},{14,37},{15,38},{62,53},{63,54},{46,69},{47,70},{9... | collective-permute-start | bytes 1572872 | tf_op jit(solution)/shard_map/ppermute | solution.py:447
  115.2 12.6 %collective-permute-start.15 = (f32[2,256,256]{2,1,0:T(8,128)S(1)}, f32[2,256,256]{2,1,0:T(8,128)S(1)}, u32[]{:S(2)}, u32[]{:S(2)}) collective-permute-start(f32[2,256,256]{2,1,0:T(8,128)S(1)} %collective-permute-done.10.refs_3_), channel_id=1, source_target_pairs={{0,8},{3,11},{4,12},{7,15},{8,16},{9,1},{10,2},{11,19},{13,5},{14,... | collective-permute-start | bytes 1572872 | tf_op jit(solution)/shard_map/ppermute | solution.py:447
  121.6 17.3 %collective-permute-start.16 = (f32[2,256,256]{2,1,0:T(8,128)S(1)}, f32[2,256,256]{2,1,0:T(8,128)S(1)}, u32[]{:S(2)}, u32[]{:S(2)}) collective-permute-start(f32[2,256,256]{2,1,0:T(8,128)S(1)} %collective-permute-done.11.refs_4_), channel_id=1, source_target_pairs={{0,8},{1,9},{4,12},{5,13},{8,16},{9,17},{10,2},{11,3},{14,6},{15,7... | collective-permute-start | bytes 1572872 | tf_op jit(solution)/shard_map/ppermute | solution.py:447
  123.5 15.4 %collective-permute-start.17 = (f32[2,256,256]{2,1,0:T(8,128)S(1)}, f32[2,256,256]{2,1,0:T(8,128)S(1)}, u32[]{:S(2)}, u32[]{:S(2)}) collective-permute-start(f32[2,256,256]{2,1,0:T(8,128)S(1)} %collective-permute-done.12.refs_5_), channel_id=1, source_target_pairs={{1,9},{2,10},{5,13},{6,14},{8,0},{9,17},{10,18},{11,3},{12,4},{15,... | collective-permute-start | bytes 1572872 | tf_op jit(solution)/shard_map/ppermute | solution.py:447
